TPU v7x, 128 devices: a whole 4x4x4 slice. The times are simulated.
128 devices in a mesh: dp: 16 (over y_lo, x, core), expert: 8 (over y_hi, z).
Axes of the slice: x: 4, y: 4 (y_hi: 2, y_lo: 2; y = y_hi * 2 + y_lo), z: 4, core: 2. Of those that a mesh axis runs over, the one named last changes fastest.
Arguments:
- out_grad: bfloat16 [16384, 6144], P(('dp', 'expert')), may hold values from -6 to 6
- routes: int32 [16384, 2], P(('dp', 'expert')), may hold values from 0 to 7, all different within a row; in each aligned block of 128 rows (0 to 127, 128 to 255, ...) at most 96 rows name the same one
- probs: bfloat16 [16384, 2], P(('dp', 'expert')), may hold values from 0.099609375 to 0.8984375
- gate_saved: bfloat16 [98304, 1024], P(('dp', 'expert')), may hold values from -6 to 6
- up_saved: bfloat16 [98304, 1024], P(('dp', 'expert')), may hold values from -6 to 6
- weight: float32 [8, 6144, 1024], P('expert', 'dp'), may hold values from -0.078125 to 0.078125
- moment1: float32 [8, 6144, 1024], P('expert', 'dp'), may hold values from -6 to 6
- moment2: float32 [8, 6144, 1024], P('expert', 'dp'), may hold values from 0.5 to 4
Outputs:
- new_weight: float32 [8, 6144, 1024], P('expert', 'dp')
- new_moment1: float32 [8, 6144, 1024], P('expert', 'dp')
- new_moment2: float32 [8, 6144, 1024], P('expert', 'dp')
- gate_grad: bfloat16 [98304, 1024], P(('dp', 'expert'))
- up_grad: bfloat16 [98304, 1024], P(('dp', 'expert'))
- prob_grad: float32 [16384, 2], P(('dp', 'expert'))
Inputs may be any that keep to these rules, and one draw needn't show every extreme that they name: `routes`: each row names 2 different experts; every expert is named somewhere. Among the rows of one device no expert is named by more than 96 rows, and in every draw some device names some expert exactly 96 times.
All inputs are finite; a program needn't handle non-finite values.
Results may differ from a plain program's by a relative error of at most 0.008.
Values may be sent and summed in bfloat16 or wider, within the bound.
No kernel may reach another device: no remote copies, remote signals or barrier semaphores. Data moves between devices by JAX's collectives and lax.ppermute only.
A program may use at most 128 MiB of HBM per device.

v0:
```python
import jax
import jax.numpy as jnp
from jax import lax
from jax.sharding import PartitionSpec as P

first_decay = 0.9
second_decay = 0.95
learn_rate = 0.01
weight_decay = 0.1
epsilon = 1e-08
first_correction = 1.0 - 0.9**20
second_correction = 1.0 - 0.95**20


def slot_tables(route_block, prob_block, experts, capacity):
    tokens_here = route_block.shape[0]
    chosen = (
        route_block[:, :, None] == jnp.arange(experts, dtype=jnp.int32)[None, None, :]
    ).astype(jnp.int32)
    per_token = jnp.sum(chosen, axis=1)
    earlier = jnp.cumsum(per_token, axis=0) - per_token
    ranking = jnp.sum(chosen * earlier[:, None, :], axis=2)
    slot_ids = route_block * capacity + ranking
    flat_slots = slot_ids.reshape(-1)
    token_ids = jnp.repeat(jnp.arange(tokens_here, dtype=jnp.int32), route_block.shape[1])
    token_of_slot = (
        jnp.full((experts * capacity,), tokens_here, jnp.int32).at[flat_slots].set(token_ids)
    )
    prob_of_slot = (
        jnp.zeros((experts * capacity,), prob_block.dtype)
        .at[flat_slots]
        .set(prob_block.reshape(-1))
    )
    return (
        slot_ids,
        token_of_slot.reshape(experts, capacity),
        prob_of_slot.reshape(experts, capacity),
    )


def on_device(out_grad, routes, probs, gate_saved, up_saved, weight, moment1, moment2):
    experts = lax.axis_size("expert")
    groups = lax.axis_size("dp")
    capacity = gate_saved.shape[0] // experts
    model_width = out_grad.shape[1]
    slot_ids, token_of_slot, prob_of_slot = slot_tables(routes, probs, experts, capacity)
    sent_rows = jnp.take(
        out_grad, token_of_slot.reshape(-1), axis=0, mode="fill", fill_value=0
    ).reshape(experts, capacity, model_width)
    arrived, arrived_prob = (
        lax.all_to_all(sent_rows, "expert", split_axis=0, concat_axis=0, tiled=True),
        lax.all_to_all(prob_of_slot, "expert", split_axis=0, concat_axis=0, tiled=True),
    )
    slot_rows = arrived.reshape(experts * capacity, model_width)
    slot_scale = arrived_prob.reshape(-1).astype(jnp.float32)
    gate_value = gate_saved.astype(jnp.float32)
    up_value = up_saved.astype(jnp.float32)
    sigmoid_gate = jax.nn.sigmoid(gate_value)
    silu_gate = gate_value * sigmoid_gate
    hidden_low = (silu_gate * up_value).astype(jnp.bfloat16)
    weight_low = weight[0].astype(jnp.bfloat16)
    columns = slot_rows
    back_grad = jnp.dot(
        columns,
        lax.all_gather(weight_low, "dp", axis=0, tiled=True),
        preferred_element_type=jnp.float32,
    )
    slot_prob_grad = jnp.sum(hidden_low.astype(jnp.float32) * back_grad, axis=1)
    hidden_grad = slot_scale[:, None] * back_grad
    gate_grad = (
        hidden_grad * up_value * sigmoid_gate * (1.0 + gate_value * (1.0 - sigmoid_gate))
    ).astype(jnp.bfloat16)
    up_grad = (hidden_grad * silu_gate).astype(jnp.bfloat16)
    returned = lax.all_to_all(
        slot_prob_grad.reshape(experts, capacity), "expert", split_axis=0, concat_axis=0, tiled=True
    )
    prob_grad = jnp.take(returned.reshape(-1), slot_ids.reshape(-1), axis=0).reshape(slot_ids.shape)
    scaled_rows = (slot_rows.astype(jnp.float32) * slot_scale[:, None]).astype(jnp.bfloat16)
    columns = scaled_rows
    grad_sum = lax.psum_scatter(
        lax.dot_general(
            columns, hidden_low, (((0,), (0,)), ((), ())), preferred_element_type=jnp.float32
        ).astype(jnp.bfloat16),
        "dp",
        scatter_dimension=0,
        tiled=True,
    ).astype(jnp.float32)
    gradient = grad_sum / groups
    master = weight[0]
    new_first = first_decay * moment1[0] + (1.0 - first_decay) * gradient
    new_second = second_decay * moment2[0] + (1.0 - second_decay) * gradient * gradient
    update = new_first / first_correction / (jnp.sqrt(new_second / second_correction) + epsilon)
    new_weight = master - learn_rate * (update + weight_decay * master)
    return (new_weight[None], new_first[None], new_second[None], gate_grad, up_grad, prob_grad)


def solution(mesh):
    placed = (
        P(("dp", "expert"), None),
        P(("dp", "expert"), None),
        P(("dp", "expert"), None),
        P(("dp", "expert"), None),
        P(("dp", "expert"), None),
        P("expert", "dp", None),
        P("expert", "dp", None),
        P("expert", "dp", None),
    )
    return jax.shard_map(
        on_device,
        mesh=mesh,
        in_specs=placed,
        out_specs=(
            P("expert", "dp", None),
            P("expert", "dp", None),
            P("expert", "dp", None),
            P(("dp", "expert"), None),
            P(("dp", "expert"), None),
            P(("dp", "expert"), None),
        ),
        check_vma=False,
    )
```

profile of v0, /device:TPU:0, one launch (start us, length us, event | category | flops | bytes accessed | tf_op | source)
XLA Modules:
  0.0 296.3 jit_solution(14565295880313098649)
XLA Ops:
  7.2 2.5 bitcast_convert_fusion
  9.8 0.1 copy.26
  9.9 0.2 reduce_window_sum.11
  10.2 0.1 copy.29
  10.3 0.1 reshape.108
  10.5 0.1 copy.30
  10.6 0.1 reshape.142
  10.8 2.2 scatter_custom_fusion.1
  12.9 0.7 all_to_all.20
  13.6 8.0 %all-to-all-start.1 = ((bf16[8,1,96]{2,1,0:T(2,128)(2,1)}), bf16[8,1,96]{2,1,0:T(2,128)(2,1)S(1)}, u32[]{:S(2)}, u32[]{:S(2)}) async-start(bf16[8,1,96]{2,1,0:T(2,128)(2,1)} %all_to_all.20), calls=%async_computation.1 | async-start | bytes 8192 | tf_op jit(solution)/shard_map/all_to_all | solution.py:52
  21.6 0.1 reshape.134
  21.8 1.4 scatter_custom_fusion
  23.2 0.1 broadcast_in_dim.47
  23.3 8.1 %gather_fusion = bf16[768,6144]{1,0:T(8,128)(2,1)} fusion(bf16[128,6144]{1,0:T(8,128)(2,1)S(1)} %copy-done, s32[1024]{0:T(1024)S(1)} %pad_clamp_fusion.1), kind=kCustom, calls=%fused_computation | custom fusion | bytes 18877440 | tf_op jit(solution)/shard_map/jit(_take)/gather | solution.py:47
  31.4 8.1 %broadcast_select_fusion = bf16[8,96,6144]{2,1,0:T(8,128)(2,1)} fusion(bf16[8,96,6144]{2,1,0:T(8,128)(2,1)} %bitcast.35, pred[8,96]{1,0:T(8,128)(4,1)S(1)} %broadcast_in_dim.47), kind=kLoop, calls=%fused_computation.7 | loop fusion | flops 4718592 | bytes 18875136 | tf_op jit(solution)/shard_map/jit(_take)/select_n | solution.py:47
  39.5 7.2 %all-to-all-start = ((bf16[8,96,6144]{2,1,0:T(8,128)(2,1)}), bf16[8,96,6144]{2,1,0:T(8,128)(2,1)}, u32[]{:S(2)}, u32[]{:S(2)}) async-start(bf16[8,96,6144]{2,1,0:T(8,128)(2,1)} %broadcast_select_fusion), calls=%async_computation | async-start | bytes 18874368 | tf_op jit(solution)/shard_map/all_to_all | solution.py:51
  46.7 0.2 reduce-scatter.2.cloned.1.call-start
  47.0 0.1 reshape.113
  47.0 138.6 %all-to-all-done = bf16[8,96,6144]{2,1,0:T(8,128)(2,1)} async-done(((bf16[8,96,6144]{2,1,0:T(8,128)(2,1)}), bf16[8,96,6144]{2,1,0:T(8,128)(2,1)}, u32[]{:S(2)}, u32[]{:S(2)}) %all-to-all-start) | async-done | bytes 9437216 | tf_op jit(solution)/shard_map/all_to_all | solution.py:51
  185.7 16.7 %convolution_convert_fusion = bf16[6144,1024]{1,0:T(8,128)(2,1)} fusion(bf16[768,6144]{1,0:T(8,128)(2,1)} %bitcast.4, f32[768]{0:T(1024)S(1)} %reshape.113, bf16[768,1024]{1,0:T(8,128)(2,1)} %param.12, bf16[768,1024]{1,0:T(8,128)(2,1)} %param.11), kind=kOutput, calls=%fused_computation.5 | convolution fusion | flops 9690415104 | bytes 25168896 | tf_op jit(solution)/shard_map/dot_general | solution.py:81
  202.4 19.1 %multiply_reduce_fusion = (f32[768]{0:T(1024)S(1)}, bf16[768,1024]{1,0:T(8,128)(2,1)}, bf16[768,1024]{1,0:T(8,128)(2,1)}) fusion(bf16[768,1024]{1,0:T(8,128)(2,1)} %param.12, bf16[768,1024]{1,0:T(8,128)(2,1)} %param.11, f32[768]{0:T(1024)S(1)} %reshape.113, bf16[768,6144]{1,0:T(8,128)(2,1)} %bitcast.4, bf16[6144,1024]{1,0:T(8,128)(2,1)} %all-gather.2.cloned.1.call-done), kind=kOutput, calls=%fused_computation.21 | convolution fusion | flops 9680190464 | bytes 28317696 | tf_op jit(solution)/shard_map/dot_general | solution.py:63
  221.5 0.7 all_to_all.18
  222.2 4.4 %all-to-all-start.2 = ((f32[8,1,96]{2,1,0:T(1,128)}), f32[8,1,96]{2,1,0:T(1,128)S(1)}, u32[]{:S(2)}, u32[]{:S(2)}) async-start(f32[8,1,96]{2,1,0:T(1,128)} %all_to_all.18), calls=%async_computation.3 | async-start | bytes 8192 | tf_op jit(solution)/shard_map/all_to_all | solution.py:74
  226.6 7.6 %all-to-all-done.2 = f32[8,1,96]{2,1,0:T(1,128)S(1)} async-done(((f32[8,1,96]{2,1,0:T(1,128)}), f32[8,1,96]{2,1,0:T(1,128)S(1)}, u32[]{:S(2)}, u32[]{:S(2)}) %all-to-all-start.2) | async-done | bytes 3104 | tf_op jit(solution)/shard_map/all_to_all | solution.py:74
  234.2 0.5 broadcast.99
  234.7 0.7 reduce.7
  235.4 0.1 reshape.112
  235.4 1.4 gather_fusion.1
  236.8 0.1 gather.15
  237.0 0.6 and_select_fusion
  237.6 46.3 %reduce-scatter.2.cloned.1.call-done = bf16[384,1024]{1,0:T(8,128)(2,1)} async-done(((bf16[6144,1024]{1,0:T(8,128)(2,1)}), bf16[384,1024]{1,0:T(8,128)(2,1)}) %reduce-scatter.2.cloned.1.call-update) | async-done | bytes 786448 | tf_op jit(solution)/shard_map/reduce_scatter | solution.py:80
  283.9 5.6 %fusion.16 = (f32[1,384,1024]{2,1,0:T(8,128)}, f32[1,384,1024]{2,1,0:T(8,128)}, f32[1,384,1024]{2,1,0:T(8,128)}) fusion(bf16[384,1024]{1,0:T(8,128)(2,1)} %reduce-scatter.2.cloned.1.call-done, f32[1,384,1024]{2,1,0:T(8,128)} %param.15, f32[1,384,1024]{2,1,0:T(8,128)} %param.14, f32[1,384,1024]{2,1,0:T(8,128)S(1)} %copy-done.2), kind=kLoop, calls=%fused_computation.36 | loop fusion | flops 6684672 | bytes 10223616 | tf_op jit(solution)/shard_map/broadcast_in_dim | solution.py:94
  (28 shorter events, 0.3 us)
Async XLA Ops:
  7.2 16.1 %copy-start = (bf16[128,6144]{1,0:T(8,128)(2,1)S(1)}, bf16[128,6144]{1,0:T(8,128)(2,1)}, u32[]{:S(2)}) copy-start(bf16[128,6144]{1,0:T(8,128)(2,1)} %param.8) | copy-start | bytes 4718596
  7.2 2.6 copy-start.3
  7.2 3.3 %copy-start.4 = (bf16[128,2]{0,1:T(2,128)(2,1)S(1)}, bf16[128,2]{0,1:T(2,128)(2,1)}, u32[]{:S(2)}) copy-start(bf16[128,2]{0,1:T(2,128)(2,1)} %param.10) | copy-start | bytes 1540
  7.2 195.2 %all-gather.2.cloned.1.call-start = ((), (), s32[]{:S(2)}) async-start(), calls=%async_computation.5 | async-start | bytes 13369344 | tf_op jit(solution)/shard_map/all_gather | solution.py:65
  13.6 25.9 %all-to-all-start.1 = ((bf16[8,1,96]{2,1,0:T(2,128)(2,1)}), bf16[8,1,96]{2,1,0:T(2,128)(2,1)S(1)}, u32[]{:S(2)}, u32[]{:S(2)}) async-start(bf16[8,1,96]{2,1,0:T(2,128)(2,1)} %all_to_all.20), calls=%async_computation.1 | async-start | bytes 8192 | tf_op jit(solution)/shard_map/all_to_all | solution.py:52
  39.5 146.1 %all-to-all-start = ((bf16[8,96,6144]{2,1,0:T(8,128)(2,1)}), bf16[8,96,6144]{2,1,0:T(8,128)(2,1)}, u32[]{:S(2)}, u32[]{:S(2)}) async-start(bf16[8,96,6144]{2,1,0:T(8,128)(2,1)} %broadcast_select_fusion), calls=%async_computation | async-start | bytes 18874368 | tf_op jit(solution)/shard_map/all_to_all | solution.py:51
  46.7 237.2 %reduce-scatter.2.cloned.1.call-start = ((), (), s32[]{:S(2)}) async-start(), calls=%async_computation.4 | async-start | bytes 13369344 | tf_op jit(solution)/shard_map/reduce_scatter | solution.py:80
  202.4 81.6 %copy-start.2 = (f32[1,384,1024]{2,1,0:T(8,128)S(1)}, f32[1,384,1024]{2,1,0:T(8,128)}, u32[]{:S(2)}) copy-start(f32[1,384,1024]{2,1,0:T(8,128)} %param.13) | copy-start | bytes 4718596
  222.2 12.0 %all-to-all-start.2 = ((f32[8,1,96]{2,1,0:T(1,128)}), f32[8,1,96]{2,1,0:T(1,128)S(1)}, u32[]{:S(2)}, u32[]{:S(2)}) async-start(f32[8,1,96]{2,1,0:T(1,128)} %all_to_all.18), calls=%async_computation.3 | async-start | bytes 8192 | tf_op jit(solution)/shard_map/all_to_all | solution.py:74
  237.0 52.5 %copy-start.1 = (bf16[128,6144]{1,0:T(8,128)(2,1)S(1)}, bf16[128,6144]{1,0:T(8,128)(2,1)}, u32[]{:S(2)}) copy-start(bf16[128,6144]{1,0:T(8,128)(2,1)} %param.8) | copy-start | bytes 4718596
Sparse Core Ops, SparseCore 0:
  10.3 109.3 all-gather.1
  202.5 81.3 reduce-scatter.1
where the time goes:
time: 297 us; the launch traced here: 296 us
  waiting for transfers between devices  193 us (65%)
  matrix products  35.8 us (12%)
  starting transfers between devices  19.9 us (7%)
  other arithmetic  17.7 us (6%)
  local copies, waits for them, and re-layouts  16.2 us (5%)
  between operations  14.2 us (5%)
    all_to_all x1, waiting for transfers between devices, on_device(): lax.all_to_all(sent_rows, 'expert', split_axis=0, concat_axis=0, tiled=True)  139 us
    reduce_scatter x1, waiting for transfers between devices, on_device(): lax.psum_scatter(lax.dot_general(columns, hidden_low, (((0,), (0,)), ((),...  46.3 us
    dot_general x1, matrix products, on_device(): jnp.dot(columns, lax.all_gather(weight_low, 'dp', axis=0, tiled=True), pr...  19.1 us
    dot_general x1, matrix products, on_device(): lax.dot_general(columns, hidden_low, (((0,), (0,)), ((), ())), preferred_...  16.7 us
    select_n x2, other arithmetic, on_device(): jnp.take(out_grad, token_of_slot.reshape(-1), axis=0, mode='fill', fill_v...  8.15 us
    gather x1, local copies, waits for them, and re-layouts, on_device(): jnp.take(out_grad, token_of_slot.reshape(-1), axis=0, mode='fill', fill_v...  8.07 us
    all_to_all x1, starting transfers between devices, on_device(): lax.all_to_all(prob_of_slot, 'expert', split_axis=0, concat_axis=0, tiled...  8.03 us
    all_to_all x1, waiting for transfers between devices, on_device(): lax.all_to_all(slot_prob_grad.reshape(experts, capacity), 'expert', split...  7.62 us
  transfers between devices with their start and end apart: 5, of which 3 were waited for; matrix products, arithmetic and copies ran while one was open for 20% of the time, Pallas kernels for 0%

commit v1 on v0

v1 whole, which is shorter than its diff:
```python
import jax
import jax.numpy as jnp
from jax import lax
from jax.experimental import pallas as pl
from jax.experimental.pallas import tpu as pltpu
from jax.sharding import PartitionSpec as P

first_decay = 0.9
second_decay = 0.95
learn_rate = 0.01
weight_decay = 0.1
epsilon = 1e-08
first_correction = 1.0 - 0.9**20
second_correction = 1.0 - 0.95**20

AXES = ("dp", "expert")
EXPERTS = 8
GROUPS = 16
TOK = 128
CAP = 96
FF = 1024
ROWS = 384
CHUNKS = 3
PART = 128
WIDE = 8 * PART


def device_id(x, y, z, core):
    return ((y % 2) * 8 + x * 2 + core) * EXPERTS + (y // 2) * 4 + z


def pairs(move):
    found = []
    for x in range(4):
        for y in range(4):
            for z in range(4):
                for core in range(2):
                    nx, ny, nz, ncore = move(x, y, z, core)
                    found.append(
                        (device_id(x, y, z, core), device_id(nx % 4, ny % 4, nz % 4, ncore))
                    )
    return found


Z_RING = pairs(lambda x, y, z, c: (x, y, z + 1 - 2 * c, c))
X_RING = pairs(lambda x, y, z, c: (x + 1 - 2 * c, y, z, c))
Y_HALF = pairs(lambda x, y, z, c: (x, y + 2, z, c))
Y_PAIR = pairs(lambda x, y, z, c: (x, y ^ 1, z, c))
CORE = pairs(lambda x, y, z, c: (x, y, z, 1 - c))


def send(value, route):
    return lax.ppermute(value, AXES, route)


def after(value, *others):
    return lax.optimization_barrier((value, *others))[0]


def split_columns(out_grad, blocks):
    def body(blocks_ref, own_in_ref, other_in_ref, *outs):
        for chunk in range(CHUNKS):
            outs[chunk][...] = own_in_ref[:, chunk * PART : (chunk + 1) * PART]
            outs[CHUNKS][chunk] = other_in_ref[:, chunk * PART : (chunk + 1) * PART]

    chunk_spec = pl.BlockSpec((TOK, PART), lambda b, o: (0, b))
    chunk_shape = jax.ShapeDtypeStruct((TOK, WIDE), out_grad.dtype)
    return pl.pallas_call(
        body,
        out_shape=[chunk_shape] * CHUNKS
        + [jax.ShapeDtypeStruct((CHUNKS, TOK, WIDE), out_grad.dtype)],
        grid_spec=pltpu.PrefetchScalarGridSpec(
            num_scalar_prefetch=1,
            grid=(8,),
            in_specs=[
                pl.BlockSpec((TOK, ROWS), lambda b, o: (0, o[b])),
                pl.BlockSpec((TOK, ROWS), lambda b, o: (0, o[8 + b])),
            ],
            out_specs=[chunk_spec] * CHUNKS
            + [pl.BlockSpec((CHUNKS, TOK, PART), lambda b, o: (0, 0, b))],
        ),
        name="split_columns",
    )(blocks, out_grad, out_grad)


def hidden_of(gate, up):
    sigmoid = 1.0 / (1.0 + jnp.exp(-gate))
    silu = gate * sigmoid
    return sigmoid, silu, (silu * up).astype(jnp.bfloat16)


def one_hot(rank_row):
    slots = lax.broadcasted_iota(jnp.int32, (CAP, TOK), 0).astype(jnp.float32)
    return slots == rank_row.astype(jnp.float32)


def token_hidden(order, gate_saved, up_saved, ranks, scales):
    def body(order_ref, gate_ref, up_ref, rank_ref, scale_ref, out_ref):
        _, _, hidden = hidden_of(
            gate_ref[...].astype(jnp.float32), up_ref[...].astype(jnp.float32)
        )
        hot = one_hot(rank_ref[0])
        mixing = jnp.where(hot, scale_ref[0].astype(jnp.float32), 0.0).astype(jnp.bfloat16)
        out_ref[0] = lax.dot_general(
            mixing, hidden, (((0,), (0,)), ((), ())), preferred_element_type=jnp.float32
        ).astype(jnp.bfloat16)

    return pl.pallas_call(
        body,
        out_shape=jax.ShapeDtypeStruct((EXPERTS, TOK, FF), jnp.bfloat16),
        grid_spec=pltpu.PrefetchScalarGridSpec(
            num_scalar_prefetch=1,
            grid=(EXPERTS,),
            in_specs=[
                pl.BlockSpec((CAP, FF), lambda r, o: (o[r], 0)),
                pl.BlockSpec((CAP, FF), lambda r, o: (o[r], 0)),
                pl.BlockSpec((1, 1, TOK), lambda r, o: (o[r], 0, 0)),
                pl.BlockSpec((1, 1, TOK), lambda r, o: (o[r], 0, 0)),
            ],
            out_specs=pl.BlockSpec((1, TOK, FF), lambda r, o: (r, 0, 0)),
        ),
        name="token_hidden",
    )(order, gate_saved, up_saved, ranks, scales)


def slot_grads(order, gate_saved, up_saved, ranks, scales, back_here, back_there):
    def body(
        order_ref, gate_ref, up_ref, rank_ref, scale_ref, here_ref, there_ref, gg_ref, ug_ref, pg_ref
    ):
        gate = gate_ref[...].astype(jnp.float32)
        up = up_ref[...].astype(jnp.float32)
        sigmoid, silu, hidden = hidden_of(gate, up)
        hot = one_hot(rank_ref[0])
        mixing = hot.astype(jnp.bfloat16)
        rows = here_ref[0] + there_ref[0]
        high = rows.astype(jnp.bfloat16)
        low = (rows - high.astype(jnp.float32)).astype(jnp.bfloat16)
        back = jnp.dot(mixing, high, preferred_element_type=jnp.float32) + jnp.dot(
            mixing, low, preferred_element_type=jnp.float32
        )
        scale = jnp.sum(
            jnp.where(hot, scale_ref[0].astype(jnp.float32), 0.0), axis=1, keepdims=True
        )
        prob = jnp.sum(hidden.astype(jnp.float32) * back, axis=1, keepdims=True)
        pg_ref[0] = jnp.sum(jnp.where(hot, prob, 0.0), axis=0, keepdims=True)
        grad = scale * back
        gg_ref[...] = (grad * up * sigmoid * (1.0 + gate * (1.0 - sigmoid))).astype(jnp.bfloat16)
        ug_ref[...] = (grad * silu).astype(jnp.bfloat16)

    slot_spec = pl.BlockSpec((CAP, FF), lambda r, o: (o[r], 0))
    row_spec = pl.BlockSpec((1, 1, TOK), lambda r, o: (o[r], 0, 0))
    tok_spec = pl.BlockSpec((1, TOK, FF), lambda r, o: (r, 0, 0))
    mirror_spec = pl.BlockSpec((1, TOK, FF), lambda r, o: (r // 4 * 4 + (4 - r % 4) % 4, 0, 0))
    slots = jax.ShapeDtypeStruct((EXPERTS * CAP, FF), jnp.bfloat16)
    return pl.pallas_call(
        body,
        out_shape=(slots, slots, jax.ShapeDtypeStruct((EXPERTS, 1, TOK), jnp.float32)),
        grid_spec=pltpu.PrefetchScalarGridSpec(
            num_scalar_prefetch=1,
            grid=(EXPERTS,),
            in_specs=[slot_spec, slot_spec, row_spec, row_spec, tok_spec, mirror_spec],
            out_specs=(slot_spec, slot_spec, row_spec),
        ),
        name="slot_grads",
    )(order, gate_saved, up_saved, ranks, scales, back_here, back_there)


def ring_steps(value, route, tie=()):
    found = []
    for step in range(3):
        value = send(after(value, *tie) if step == 0 and tie else value, route)
        found.append(value)
    return found


def add(*terms):
    return sum(term.astype(jnp.float32) for term in terms)


def reduce_ring(blocks):
    value = blocks[1]
    for step in range(3):
        met = send(value, X_RING)
        if step == 2:
            return add(met, blocks[0])
        value = add(met, blocks[step + 2]).astype(jnp.bfloat16)


def on_device(out_grad, routes, probs, gate_saved, up_saved, weight, moment1, moment2):
    place = lax.axis_index("dp")
    expert = lax.axis_index("expert")
    y_low, x, core = place // 8, (place // 2) % 4, place % 2
    y_high, z = expert // 4, expert % 4

    blocks = jnp.stack(
        [
            ((y_low ^ dy) * 4 + (x - k * (1 - 2 * side)) % 4) * 2 + side
            for side in (core, 1 - core)
            for k in range(4)
            for dy in range(2)
        ]
    ).astype(jnp.int32)
    order = jnp.stack(
        [
            (y_high ^ dy) * 4 + (z - k * (1 - 2 * core)) % 4
            for dy in range(2)
            for k in range(4)
        ]
    ).astype(jnp.int32)

    *own_columns, other_columns = split_columns(out_grad, blocks)
    met = send(other_columns, CORE)
    here = [jnp.concatenate([own_columns[chunk], met[chunk]]) for chunk in range(CHUNKS)]

    weight_low = weight[0].astype(jnp.bfloat16)
    weight_pair = send(weight_low, Y_PAIR)
    near = [weight_low, *ring_steps(weight_low, X_RING)]
    far = [weight_pair, *ring_steps(weight_pair, X_RING)]

    first_half = [here[0]]
    first_half.append(send(here[0], Z_RING))
    pair_one = send(here[1], Y_HALF)
    both_one = [after(jnp.stack([here[1], pair_one]), first_half[1])]
    first_half.append(send(first_half[1], Z_RING))
    first_half.append(send(first_half[2], Z_RING))
    both_one += ring_steps(both_one[0], Z_RING)
    pair_two = send(after(here[2], pair_one), Y_HALF)
    both_two = [after(jnp.stack([here[2], pair_two]), first_half[3])]
    both_two += ring_steps(both_two[0], Z_RING)
    whole_half = jnp.stack(first_half)
    whole_half = jnp.stack([whole_half, send(after(whole_half, pair_two), Y_HALF)])

    tokens = [
        whole_half.reshape(EXPERTS * 2 * TOK, WIDE),
        jnp.stack(both_one, axis=1).reshape(EXPERTS * 2 * TOK, WIDE),
        jnp.stack(both_two, axis=1).reshape(EXPERTS * 2 * TOK, WIDE),
    ]

    member = jnp.sum(
        (routes[:, :, None] == jnp.arange(EXPERTS, dtype=jnp.int32)).astype(jnp.float32), axis=1
    )
    earlier = jnp.tril(jnp.ones((TOK, TOK), jnp.float32), -1)
    rank = jnp.dot(earlier, member)
    rank = jnp.where(member > 0, rank, -1.0)
    share = jnp.sum(
        jnp.where(
            routes[:, :, None] == jnp.arange(EXPERTS, dtype=jnp.int32),
            probs[:, :, None].astype(jnp.float32),
            0.0,
        ),
        axis=1,
    )
    notes = jnp.stack([rank.T, share.T], axis=1).astype(jnp.bfloat16)
    notes = lax.all_to_all(
        after(notes, first_half[1]), "expert", split_axis=0, concat_axis=0, tiled=True
    )
    ranks, scales = notes[:, 0:1], notes[:, 1:2]

    hidden_here = token_hidden(order, gate_saved, up_saved, ranks, scales)
    hidden_there = send(hidden_here, CORE)
    mirror = [dy * 4 + (4 - k) % 4 for dy in range(2) for k in range(4)]
    hidden = jnp.stack(
        [hidden_here, jnp.stack([hidden_there[r] for r in mirror])], axis=1
    ).reshape(EXPERTS * 2 * TOK, FF)

    gathered = jnp.stack([w[k] for k in range(4) for w in (near, far)])
    tokens[1], gathered = lax.optimization_barrier((tokens[1], gathered))

    sums = [None] * CHUNKS
    for chunk in (1, 0, 2):
        product = lax.dot_general(
            tokens[chunk], hidden, (((0,), (0,)), ((), ())), preferred_element_type=jnp.float32
        ).astype(jnp.bfloat16)
        product = product.reshape(4, 2, PART, FF)
        if chunk == 2:
            other = reduce_ring([product[k, 1] for k in range(4)]).astype(jnp.bfloat16)
            mine = reduce_ring([product[k, 0] for k in range(4)])
        else:
            mine, other = reduce_ring([product[k] for k in range(4)])
            other = other.astype(jnp.bfloat16)
        sums[chunk] = mine + send(other, Y_PAIR).astype(jnp.float32)

    back = sum(
        jnp.dot(
            tokens[chunk],
            gathered[:, chunk * PART : (chunk + 1) * PART].reshape(WIDE, FF),
            preferred_element_type=jnp.float32,
        )
        for chunk in (1, 0, 2)
    ).reshape(EXPERTS, 2, TOK, FF)
    back_there = send(back[:, 1], CORE)
    gate_grad, up_grad, prob_rows = slot_grads(
        order, gate_saved, up_saved, ranks, scales, back[:, 0], back_there
    )
    returned = lax.all_to_all(
        prob_rows, "expert", split_axis=0, concat_axis=0, tiled=True
    ).reshape(EXPERTS, TOK)
    prob_grad = jnp.sum(
        jnp.where(
            routes[:, :, None] == jnp.arange(EXPERTS, dtype=jnp.int32), returned.T[:, None, :], 0.0
        ),
        axis=2,
    )

    gradient = jnp.concatenate(sums, axis=0) / GROUPS
    master = weight[0]
    new_first = first_decay * moment1[0] + (1.0 - first_decay) * gradient
    new_second = second_decay * moment2[0] + (1.0 - second_decay) * gradient * gradient
    update = new_first / first_correction / (jnp.sqrt(new_second / second_correction) + epsilon)
    new_weight = master - learn_rate * (update + weight_decay * master)
    return (new_weight[None], new_first[None], new_second[None], gate_grad, up_grad, prob_grad)


def solution(mesh):
    rows = P(("dp", "expert"), None)
    states = P("expert", "dp", None)
    return jax.shard_map(
        on_device,
        mesh=mesh,
        in_specs=(rows, rows, rows, rows, rows, states, states, states),
        out_specs=(states, states, states, rows, rows, rows),
        check_vma=False,
    )
```

time: 297 us -> 262 us (0.88)
  waiting for transfers between devices: 193 us -> 105 us
  Pallas kernels: 0 us -> 24.6 us
  starting transfers between devices: 19.9 us -> 44 us
  between operations: 14.2 us -> 1.34 us
  other arithmetic: 17.7 us -> 25.7 us
  local copies, waits for them, and re-layouts: 16.2 us -> 22.8 us
    all_to_all x3 -> x2, waiting for transfers between devices: 146 us -> 4.09 us  [the longest x1 2.49 us: on_device(): lax.all_to_all(prob_rows, 'expert', split_axis=0, concat_axis=0, tiled=True)]
    ppermute x0 -> x37, waiting for transfers between devices: none -> 101 us  [send(): return lax.ppermute(value, AXES, route)]
    reduce_scatter x1 -> x0, waiting for transfers between devices: 46.3 us -> none  [on_device(): lax.psum_scatter(lax.dot_general(columns, hidden_low, (((0,), (0,)), ((),...]
    ppermute x0 -> x37, starting transfers between devices: none -> 32.7 us  [send(): return lax.ppermute(value, AXES, route)]
    pallas_call x0 -> x3, Pallas kernels: none -> 24.6 us  [the longest x1 10.5 us: slot_grads(): pl.pallas_call(body, out_shape=(slots, slots, jax.ShapeDtypeStruct((EXPER...]
    another operation x1 -> x11, other arithmetic: 0.17 us -> 12.3 us  [the longest x2 3.51 us: on_device(): jnp.stack([whole_half, send(after(whole_half, pair_two), Y_HALF)])]
    unnamed x11 -> x43, local copies, waits for them, and re-layouts: 0.17 us -> 11.5 us
    gather x4 -> x0, local copies, waits for them, and re-layouts: 9.63 us -> none  [the longest x1 8.07 us: on_device(): jnp.take(out_grad, token_of_slot.reshape(-1), axis=0, mode='fill', fill_v...]
  transfers between devices with their start and end apart: 5 -> 39, of which waited for: 3 -> 18; matrix products, arithmetic and copies ran while one was open for 20% -> 31% of each run, Pallas kernels for 0% -> 3%
where the time goes in v1:
time: 262 us; the launch traced here: 260 us
  waiting for transfers between devices  105 us (40%)
  starting transfers between devices  44 us (17%)
  matrix products  36.7 us (14%)
  other arithmetic  25.7 us (10%)
  Pallas kernels  24.6 us (9%)
  local copies, waits for them, and re-layouts  22.8 us (9%)
    ppermute x37, waiting for transfers between devices, send(): return lax.ppermute(value, AXES, route)  101 us
    ppermute x37, starting transfers between devices, send(): return lax.ppermute(value, AXES, route)  32.7 us
    dot_general x3, matrix products, on_device(): jnp.dot(tokens[chunk], gathered[:, chunk * PART:(chunk + 1) * PART].resha...  22.2 us
    dot_general x3, matrix products, on_device(): lax.dot_general(tokens[chunk], hidden, (((0,), (0,)), ((), ())), preferre...  14.3 us
    unnamed x43, local copies, waits for them, and re-layouts  11.5 us
    pallas_call x1, Pallas kernels, slot_grads(): pl.pallas_call(body, out_shape=(slots, slots, jax.ShapeDtypeStruct((EXPER...  10.5 us
    all_to_all x1, starting transfers between devices, on_device(): lax.all_to_all(after(notes, first_half[1]), 'expert', split_axis=0, conca...  7.94 us
    pallas_call x1, Pallas kernels, token_hidden(): pl.pallas_call(body, out_shape=jax.ShapeDtypeStruct((EXPERTS, TOK, FF), j...  7.81 us
  transfers between devices with their start and end apart: 39, of which 18 were waited for; matrix products, arithmetic and copies ran while one was open for 31% of the time, Pallas kernels for 3%

profile of v1, /device:TPU:0, one launch (start us, length us, event | category | flops | bytes accessed | tf_op | source)
XLA Modules:
  0.0 260.4 jit_solution(8714837336149626120)
XLA Ops:
  1.5 6.4 %split_columns.1 = (bf16[128,1024]{1,0:T(8,128)(2,1)}, bf16[128,1024]{1,0:T(8,128)(2,1)}, bf16[128,1024]{1,0:T(8,128)(2,1)}, bf16[3,128,1024]{2,1,0:T(8,128)(2,1)}) custom-call(s32[16]{0:T(128)} %stack.215.blocks_ref, bf16[128,6144]{1,0:T(8,128)(2,1)} %other_in_ref.1, bf16[128,6144]{1,0:T(8,128)(2,1)} %other_in_ref.1), custom_call_target="tpu_custom_call" | custom-call | tf_op jit(solution)/shard_map/split_columns/pallas_call | solution.py:68
  12.3 2.9 %collective-permute-start.4 = (bf16[256,1024]{1,0:T(8,128)(2,1)S(1)}, bf16[256,1024]{1,0:T(8,128)(2,1)}, u32[]{:S(2)}, u32[]{:S(2)}) collective-permute-start(bf16[256,1024]{1,0:T(8,128)(2,1)S(1)} %get-tuple-element.66), channel_id=1, source_target_pairs={{0,4},{8,12},{1,5},{9,13},{2,6},{10,14},{3,7},{11,15},{64,68},{72,... | collective-permute-start | bytes 1572872 | tf_op jit(solution)/shard_map/ppermute | solution.py:53
  19.1 9.5 %collective-permute-done.15 = bf16[384,1024]{1,0:T(8,128)(2,1)} collective-permute-done((bf16[384,1024]{1,0:T(8,128)(2,1)S(1)}, bf16[384,1024]{1,0:T(8,128)(2,1)}, u32[]{:S(2)}, u32[]{:S(2)}) %collective-permute-start.15) | collective-permute-done | bytes 786464 | tf_op jit(solution)/shard_map/ppermute | solution.py:53
  33.2 7.9 %all-to-all-start = ((bf16[8,2,128]{2,1,0:T(2,128)(2,1)}), bf16[8,2,128]{2,1,0:T(2,128)(2,1)S(1)}, u32[]{:S(2)}, u32[]{:S(2)}) async-start(bf16[8,2,128]{2,1,0:T(2,128)(2,1)} %pad_maximum_fusion.11), calls=%async_computation | async-start | bytes 8192 | tf_op jit(solution)/shard_map/all_to_all | solution.py:254
  49.3 7.8 %token_hidden.1 = bf16[8,128,1024]{2,1,0:T(8,128)(2,1)} custom-call(s32[8]{0:T(128)} %stack.232.order_ref, bf16[768,1024]{1,0:T(8,128)(2,1)} %gate_ref.3, bf16[768,1024]{1,0:T(8,128)(2,1)} %up_ref.3, bf16[8,1,128]{2,1,0:T(2,128)(2,1)} %get-tuple-element.70.rank_ref, bf16[8,1,128]{2,1,0:T(2,128)(2,1)} %get-tuple-element.69.scale_ref), custom_call_target="tpu_custom_call" | custom-call | tf_op jit(solution)/shard_map/token_hidden/pallas_call | solution.py:108
  62.1 3.7 %collective-permute-done.2 = bf16[256,1024]{1,0:T(8,128)(2,1)} collective-permute-done((bf16[256,1024]{1,0:T(8,128)(2,1)}, bf16[256,1024]{1,0:T(8,128)(2,1)}, u32[]{:S(2)}, u32[]{:S(2)}) %collective-permute-start.2) | collective-permute-done | bytes 524320 | tf_op jit(solution)/shard_map/ppermute | solution.py:53
  70.0 7.6 %collective-permute-done.5 = bf16[256,1024]{1,0:T(8,128)(2,1)S(1)} collective-permute-done((bf16[256,1024]{1,0:T(8,128)(2,1)S(1)}, bf16[256,1024]{1,0:T(8,128)(2,1)S(1)}, u32[]{:S(2)}, u32[]{:S(2)}) %collective-permute-start.5) | collective-permute-done | bytes 524320 | tf_op jit(solution)/shard_map/ppermute | solution.py:53
  85.5 5.5 %collective-permute-done.20 = bf16[384,1024]{1,0:T(8,128)(2,1)S(1)} collective-permute-done((bf16[384,1024]{1,0:T(8,128)(2,1)}, bf16[384,1024]{1,0:T(8,128)(2,1)S(1)}, u32[]{:S(2)}, u32[]{:S(2)}) %collective-permute-start.20) | collective-permute-done | bytes 786464 | tf_op jit(solution)/shard_map/ppermute | solution.py:53
  91.7 7.8 %collective-permute-done.21 = bf16[384,1024]{1,0:T(8,128)(2,1)S(1)} collective-permute-done((bf16[384,1024]{1,0:T(8,128)(2,1)S(1)}, bf16[384,1024]{1,0:T(8,128)(2,1)S(1)}, u32[]{:S(2)}, u32[]{:S(2)}) %collective-permute-start.21) | collective-permute-done | bytes 786464 | tf_op jit(solution)/shard_map/ppermute | solution.py:53
  99.6 6.1 %collective-permute-done.26 = bf16[2,256,1024]{2,1,0:T(8,128)(2,1)} collective-permute-done((bf16[2,256,1024]{2,1,0:T(8,128)(2,1)S(1)}, bf16[2,256,1024]{2,1,0:T(8,128)(2,1)}, u32[]{:S(2)}, u32[]{:S(2)}) %collective-permute-start.26) | collective-permute-done | bytes 1048608 | tf_op jit(solution)/shard_map/ppermute | solution.py:53
  107.7 25.5 %collective-permute-done.14 = bf16[2,256,1024]{2,1,0:T(8,128)(2,1)S(1)} collective-permute-done((bf16[2,256,1024]{2,1,0:T(8,128)(2,1)S(1)}, bf16[2,256,1024]{2,1,0:T(8,128)(2,1)S(1)}, u32[]{:S(2)}, u32[]{:S(2)}) %collective-permute-start.14) | collective-permute-done | bytes 1048608 | tf_op jit(solution)/shard_map/ppermute | solution.py:53
  136.4 4.8 %convolution_convert_fusion.1 = bf16[1024,1024]{1,0:T(8,128)(2,1)S(1)} fusion(bf16[2048,1024]{1,0:T(8,128)(2,1)S(1)} %bitcast.187, bf16[2048,1024]{1,0:T(8,128)(2,1)S(1)} %bitcast.184), kind=kOutput, calls=%fused_computation.9 | convolution fusion | flops 4296015872 | bytes 10485760 | tf_op jit(solution)/shard_map/dot_general | solution.py:271
  145.5 4.8 %convolution_convert_fusion.2 = bf16[1024,1024]{1,0:T(8,128)(2,1)S(1)} fusion(bf16[2048,1024]{1,0:T(8,128)(2,1)S(1)} %bitcast.189, bf16[2048,1024]{1,0:T(8,128)(2,1)S(1)} %bitcast.185), kind=kOutput, calls=%fused_computation.10 | convolution fusion | flops 4296015872 | bytes 10485760 | tf_op jit(solution)/shard_map/dot_general | solution.py:271
  151.9 2.1 fusion.29
  154.1 6.7 %fusion.33 = f32[2048,1024]{1,0:T(8,128)} fusion(bf16[2048,1024]{1,0:T(8,128)(2,1)S(1)} %bitcast.188, bf16[1024,1024]{1,0:T(8,128)(2,1)S(1)} %bitcast.203), kind=kOutput, calls=%fused_computation.106 | convolution fusion | flops 4294967296 | bytes 14680064 | tf_op jit(solution)/shard_map/dot_general | solution.py:284
  160.8 6.6 %fusion.34 = f32[2048,1024]{1,0:T(8,128)} fusion(bf16[2048,1024]{1,0:T(8,128)(2,1)S(1)} %bitcast.190, bf16[1024,1024]{1,0:T(8,128)(2,1)S(1)} %bitcast.202), kind=kOutput, calls=%fused_computation.107 | convolution fusion | flops 4294967296 | bytes 14680064 | tf_op jit(solution)/shard_map/dot_general | solution.py:284
  168.4 2.7 %collective-permute-start.23 = (bf16[2,128,1024]{2,1,0:T(8,128)(2,1)}, bf16[2,128,1024]{2,1,0:T(8,128)(2,1)}, u32[]{:S(2)}, u32[]{:S(2)}) collective-permute-start(bf16[2,128,1024]{2,1,0:T(8,128)(2,1)} %fusion.3), channel_id=1, source_target_pairs={{0,16},{8,56},{1,17},{9,57},{2,18},{10,58},{3,19},{11,59},{64,80},... | collective-permute-start | bytes 1572872 | tf_op jit(solution)/shard_map/ppermute | solution.py:53
  173.4 3.6 %collective-permute-done.28 = bf16[2,256,1024]{2,1,0:T(8,128)(2,1)S(1)} collective-permute-done((bf16[2,256,1024]{2,1,0:T(8,128)(2,1)}, bf16[2,256,1024]{2,1,0:T(8,128)(2,1)S(1)}, u32[]{:S(2)}, u32[]{:S(2)}) %collective-permute-start.28) | collective-permute-done | bytes 1048608 | tf_op jit(solution)/shard_map/ppermute | solution.py:53
  179.2 8.9 %add_add_fusion = f32[2048,1024]{1,0:T(8,128)S(1)} fusion(f32[2048,1024]{1,0:T(8,128)} %fusion.33, f32[2048,1024]{1,0:T(8,128)} %fusion.34, bf16[2048,1024]{1,0:T(8,128)(2,1)S(1)} %bitcast.191, bf16[1024,1024]{1,0:T(8,128)(2,1)} %bitcast.201), kind=kOutput, calls=%fused_computation | convolution fusion | flops 4299161600 | bytes 31457280 | tf_op jit(solution)/shard_map/dot_general | solution.py:284
  188.1 3.2 %slice_bitcast_fusion = (f32[8,128,1024]{2,1,0:T(8,128)S(1)}, f32[8,128,1024]{2,1,0:T(8,128)}) fusion(f32[8,2,128,1024]{3,2,1,0:T(8,128)S(1)} %bitcast.182), kind=kLoop, calls=%fused_computation.1 | loop fusion | bytes 16777216 | tf_op jit(solution)/shard_map/squeeze | solution.py:291
  192.8 2.8 %collective-permute-start.24 = (bf16[2,128,1024]{2,1,0:T(8,128)(2,1)S(1)}, bf16[2,128,1024]{2,1,0:T(8,128)(2,1)S(1)}, u32[]{:S(2)}, u32[]{:S(2)}) collective-permute-start(bf16[2,128,1024]{2,1,0:T(8,128)(2,1)S(1)} %fusion.2), channel_id=1, source_target_pairs={{0,16},{8,56},{1,17},{9,57},{2,18},{10,58},{3,19},{11,59},{64,80},... | collective-permute-start | bytes 1572872 | tf_op jit(solution)/shard_map/ppermute | solution.py:53
  195.5 4.8 %convolution_convert_fusion = bf16[1024,1024]{1,0:T(8,128)(2,1)S(1)} fusion(bf16[2048,1024]{1,0:T(8,128)(2,1)S(1)} %bitcast.192, bf16[2048,1024]{1,0:T(8,128)(2,1)S(1)} %bitcast.186), kind=kOutput, calls=%fused_computation.8 | convolution fusion | flops 4296015872 | bytes 10485760 | tf_op jit(solution)/shard_map/dot_general | solution.py:271
  203.7 4.3 %collective-permute-done.32 = bf16[128,1024]{1,0:T(8,128)(2,1)S(1)} collective-permute-done((bf16[128,1024]{1,0:T(8,128)(2,1)S(1)}, bf16[128,1024]{1,0:T(8,128)(2,1)S(1)}, u32[]{:S(2)}, u32[]{:S(2)}) %collective-permute-start.32) | collective-permute-done | bytes 262176 | tf_op jit(solution)/shard_map/ppermute | solution.py:53
  209.2 7.3 %collective-permute-done.29 = bf16[128,1024]{1,0:T(8,128)(2,1)S(1)} collective-permute-done((bf16[128,1024]{1,0:T(8,128)(2,1)S(1)}, bf16[128,1024]{1,0:T(8,128)(2,1)S(1)}, u32[]{:S(2)}, u32[]{:S(2)}) %collective-permute-start.29) | collective-permute-done | bytes 262176 | tf_op jit(solution)/shard_map/ppermute | solution.py:53
  216.4 2.8 %collective-permute-done.33 = bf16[128,1024]{1,0:T(8,128)(2,1)S(1)} collective-permute-done((bf16[128,1024]{1,0:T(8,128)(2,1)S(1)}, bf16[128,1024]{1,0:T(8,128)(2,1)S(1)}, u32[]{:S(2)}, u32[]{:S(2)}) %collective-permute-start.33) | collective-permute-done | bytes 262176 | tf_op jit(solution)/shard_map/ppermute | solution.py:53
  220.8 6.3 %collective-permute-done.30 = bf16[128,1024]{1,0:T(8,128)(2,1)S(1)} collective-permute-done((bf16[128,1024]{1,0:T(8,128)(2,1)S(1)}, bf16[128,1024]{1,0:T(8,128)(2,1)S(1)}, u32[]{:S(2)}, u32[]{:S(2)}) %collective-permute-start.30) | collective-permute-done | bytes 262176 | tf_op jit(solution)/shard_map/ppermute | solution.py:53
  227.1 2.8 %collective-permute-done.34 = bf16[128,1024]{1,0:T(8,128)(2,1)S(1)} collective-permute-done((bf16[128,1024]{1,0:T(8,128)(2,1)S(1)}, bf16[128,1024]{1,0:T(8,128)(2,1)S(1)}, u32[]{:S(2)}, u32[]{:S(2)}) %collective-permute-start.34) | collective-permute-done | bytes 262176 | tf_op jit(solution)/shard_map/ppermute | solution.py:53
  231.0 5.6 %collective-permute-done.35 = bf16[128,1024]{1,0:T(8,128)(2,1)S(1)} collective-permute-done((bf16[128,1024]{1,0:T(8,128)(2,1)S(1)}, bf16[128,1024]{1,0:T(8,128)(2,1)S(1)}, u32[]{:S(2)}, u32[]{:S(2)}) %collective-permute-start.35) | collective-permute-done | bytes 262176 | tf_op jit(solution)/shard_map/ppermute | solution.py:53
  238.6 10.5 %slot_grads.1 = (bf16[768,1024]{1,0:T(8,128)(2,1)}, bf16[768,1024]{1,0:T(8,128)(2,1)}, f32[8,1,128]{2,1,0:T(1,128)}) custom-call(s32[8]{0:T(128)} %stack.232.order_ref, bf16[768,1024]{1,0:T(8,128)(2,1)} %gate_ref.3, bf16[768,1024]{1,0:T(8,128)(2,1)} %up_ref.3, bf16[8,1,128]{2,1,0:T(2,128)(2,1)} %get-tuple-element.70.rank_ref, ...), custom_call_target="tpu_custom_call" | custom-call | tf_op jit(solution)/shard_map/slot_grads/pallas_call | solution.py:155
  249.0 3.3 %all-to-all-start.1 = ((f32[8,1,128]{2,1,0:T(1,128)}), f32[8,1,128]{2,1,0:T(1,128)S(1)}, u32[]{:S(2)}, u32[]{:S(2)}) async-start(f32[8,1,128]{2,1,0:T(1,128)} %get-tuple-element.33), calls=%async_computation.1 | async-start | bytes 8192 | tf_op jit(solution)/shard_map/all_to_all | solution.py:295
  252.4 4.9 %multiply_subtract_fusion = (f32[1,384,1024]{2,1,0:T(8,128)}, f32[1,384,1024]{2,1,0:T(8,128)}, f32[1,384,1024]{2,1,0:T(8,128)}) fusion(f32[1,384,1024]{2,1,0:T(8,128)S(1)} %copy-done, f32[1,128,1024]{2,1,0:T(8,128)S(1)} %fusion.14, f32[1,128,1024]{2,1,0:T(8,128)S(1)} %fusion.7, f32[1,128,1024]{2,1,0:T(8,128)S(1)} %fusion.9, f32[1,384,1024]{2,1,0:T(8,128)} %param.14, ...), kind=kLoop, calls=%fused_computation.12 | loop fusion | flops 7077888 | bytes 11010048 | tf_op jit(solution)/shard_map/sub | solution.py:310
  257.3 2.5 all-to-all-done.1
  (147 shorter events, 67.0 us)
Async XLA Ops:
  8.0 20.5 %collective-permute-start.15 = (bf16[384,1024]{1,0:T(8,128)(2,1)S(1)}, bf16[384,1024]{1,0:T(8,128)(2,1)}, u32[]{:S(2)}, u32[]{:S(2)}) collective-permute-start(bf16[384,1024]{1,0:T(8,128)(2,1)S(1)} %convert_bitcast_fusion), channel_id=1, source_target_pairs={{0,64},{8,72},{1,65},{9,73},{2,66},{10,74},{3,67},{11,75},{64,0},{... | collective-permute-start | bytes 2359304 | tf_op jit(solution)/shard_map/ppermute | solution.py:53
  9.8 20.6 %collective-permute-start.16 = (bf16[384,1024]{1,0:T(8,128)(2,1)S(1)}, bf16[384,1024]{1,0:T(8,128)(2,1)}, u32[]{:S(2)}, u32[]{:S(2)}) collective-permute-start(bf16[384,1024]{1,0:T(8,128)(2,1)S(1)} %convert_bitcast_fusion), channel_id=1, source_target_pairs={{0,16},{8,56},{1,17},{9,57},{2,18},{10,58},{3,19},{11,59},{64,80},... | collective-permute-start | bytes 2359304 | tf_op jit(solution)/shard_map/ppermute | solution.py:53
  12.3 29.6 %collective-permute-start.4 = (bf16[256,1024]{1,0:T(8,128)(2,1)S(1)}, bf16[256,1024]{1,0:T(8,128)(2,1)}, u32[]{:S(2)}, u32[]{:S(2)}) collective-permute-start(bf16[256,1024]{1,0:T(8,128)(2,1)S(1)} %get-tuple-element.66), channel_id=1, source_target_pairs={{0,4},{8,12},{1,5},{9,13},{2,6},{10,14},{3,7},{11,15},{64,68},{72,... | collective-permute-start | bytes 1572872 | tf_op jit(solution)/shard_map/ppermute | solution.py:53
  16.1 17.1 %collective-permute-start.1 = (bf16[256,1024]{1,0:T(8,128)(2,1)}, bf16[256,1024]{1,0:T(8,128)(2,1)S(1)}, u32[]{:S(2)}, u32[]{:S(2)}) collective-permute-start(bf16[256,1024]{1,0:T(8,128)(2,1)} %get-tuple-element.64), channel_id=1, source_target_pairs={{0,1},{8,11},{1,2},{9,8},{2,3},{10,9},{3,0},{11,10},{64,65},{72,75... | collective-permute-start | bytes 1572872 | tf_op jit(solution)/shard_map/ppermute | solution.py:53
  28.6 30.7 %collective-permute-start.17 = (bf16[384,1024]{1,0:T(8,128)(2,1)}, bf16[384,1024]{1,0:T(8,128)(2,1)}, u32[]{:S(2)}, u32[]{:S(2)}) collective-permute-start(bf16[384,1024]{1,0:T(8,128)(2,1)} %collective-permute-done.15), channel_id=1, source_target_pairs={{0,16},{8,56},{1,17},{9,57},{2,18},{10,58},{3,19},{11,59},{64,80},... | collective-permute-start | bytes 2359304 | tf_op jit(solution)/shard_map/ppermute | solution.py:53
  30.4 31.1 %collective-permute-start.18 = (bf16[384,1024]{1,0:T(8,128)(2,1)}, bf16[384,1024]{1,0:T(8,128)(2,1)}, u32[]{:S(2)}, u32[]{:S(2)}) collective-permute-start(bf16[384,1024]{1,0:T(8,128)(2,1)} %collective-permute-done.16), channel_id=1, source_target_pairs={{0,16},{8,56},{1,17},{9,57},{2,18},{10,58},{3,19},{11,59},{64,80},... | collective-permute-start | bytes 2359304 | tf_op jit(solution)/shard_map/ppermute | solution.py:53
  33.2 15.5 %all-to-all-start = ((bf16[8,2,128]{2,1,0:T(2,128)(2,1)}), bf16[8,2,128]{2,1,0:T(2,128)(2,1)S(1)}, u32[]{:S(2)}, u32[]{:S(2)}) async-start(bf16[8,2,128]{2,1,0:T(2,128)(2,1)} %pad_maximum_fusion.11), calls=%async_computation | async-start | bytes 8192 | tf_op jit(solution)/shard_map/all_to_all | solution.py:254
  43.2 34.8 %collective-permute-start.12 = (bf16[2,256,1024]{2,1,0:T(8,128)(2,1)S(1)}, bf16[2,256,1024]{2,1,0:T(8,128)(2,1)}, u32[]{:S(2)}, u32[]{:S(2)}) collective-permute-start(bf16[2,256,1024]{2,1,0:T(8,128)(2,1)S(1)} %pad_maximum_fusion.6), channel_id=1, source_target_pairs={{0,1},{8,11},{1,2},{9,8},{2,3},{10,9},{3,0},{11,10},{64,65},{72,75... | collective-permute-start | bytes 3145736 | tf_op jit(solution)/shard_map/ppermute | solution.py:53
  45.2 20.6 %collective-permute-start.2 = (bf16[256,1024]{1,0:T(8,128)(2,1)}, bf16[256,1024]{1,0:T(8,128)(2,1)}, u32[]{:S(2)}, u32[]{:S(2)}) collective-permute-start(bf16[256,1024]{1,0:T(8,128)(2,1)} %copy-done.9), channel_id=1, source_target_pairs={{0,1},{8,11},{1,2},{9,8},{2,3},{10,9},{3,0},{11,10},{64,65},{72,75... | collective-permute-start | bytes 1572872 | tf_op jit(solution)/shard_map/ppermute | solution.py:53
  57.2 48.8 %collective-permute-start.7 = (bf16[8,128,1024]{2,1,0:T(8,128)(2,1)}, bf16[8,128,1024]{2,1,0:T(8,128)(2,1)S(1)}, u32[]{:S(2)}, u32[]{:S(2)}) collective-permute-start(bf16[8,128,1024]{2,1,0:T(8,128)(2,1)} %token_hidden.1), channel_id=1, source_target_pairs={{0,8},{8,0},{1,9},{9,1},{2,10},{10,2},{3,11},{11,3},{64,72},{72,64... | collective-permute-start | bytes 6291464 | tf_op jit(solution)/shard_map/ppermute | solution.py:53
  59.2 20.0 %collective-permute-start.19 = (bf16[384,1024]{1,0:T(8,128)(2,1)}, bf16[384,1024]{1,0:T(8,128)(2,1)S(1)}, u32[]{:S(2)}, u32[]{:S(2)}) collective-permute-start(bf16[384,1024]{1,0:T(8,128)(2,1)} %collective-permute-done.17), channel_id=1, source_target_pairs={{0,16},{8,56},{1,17},{9,57},{2,18},{10,58},{3,19},{11,59},{64,80},... | collective-permute-start | bytes 2359304 | tf_op jit(solution)/shard_map/ppermute | solution.py:53
  61.5 16.2 %collective-permute-start.5 = (bf16[256,1024]{1,0:T(8,128)(2,1)S(1)}, bf16[256,1024]{1,0:T(8,128)(2,1)S(1)}, u32[]{:S(2)}, u32[]{:S(2)}) collective-permute-start(bf16[256,1024]{1,0:T(8,128)(2,1)S(1)} %get-tuple-element.24), channel_id=1, source_target_pairs={{0,4},{8,12},{1,5},{9,13},{2,6},{10,14},{3,7},{11,15},{64,68},{72,... | collective-permute-start | bytes 1572872 | tf_op jit(solution)/shard_map/ppermute | solution.py:53
  65.8 12.8 %collective-permute-start.3 = (bf16[256,1024]{1,0:T(8,128)(2,1)}, bf16[256,1024]{1,0:T(8,128)(2,1)S(1)}, u32[]{:S(2)}, u32[]{:S(2)}) collective-permute-start(bf16[256,1024]{1,0:T(8,128)(2,1)} %collective-permute-done.2), channel_id=1, source_target_pairs={{0,1},{8,11},{1,2},{9,8},{2,3},{10,9},{3,0},{11,10},{64,65},{72,75... | collective-permute-start | bytes 1572872 | tf_op jit(solution)/shard_map/ppermute | solution.py:53
  77.7 13.4 %collective-permute-start.20 = (bf16[384,1024]{1,0:T(8,128)(2,1)}, bf16[384,1024]{1,0:T(8,128)(2,1)S(1)}, u32[]{:S(2)}, u32[]{:S(2)}) collective-permute-start(bf16[384,1024]{1,0:T(8,128)(2,1)} %collective-permute-done.18), channel_id=1, source_target_pairs={{0,16},{8,56},{1,17},{9,57},{2,18},{10,58},{3,19},{11,59},{64,80},... | collective-permute-start | bytes 2359304 | tf_op jit(solution)/shard_map/ppermute | solution.py:53
  78.0 27.6 %collective-permute-start.13 = (bf16[2,256,1024]{2,1,0:T(8,128)(2,1)}, bf16[2,256,1024]{2,1,0:T(8,128)(2,1)S(1)}, u32[]{:S(2)}, u32[]{:S(2)}) collective-permute-start(bf16[2,256,1024]{2,1,0:T(8,128)(2,1)} %collective-permute-done.12), channel_id=1, source_target_pairs={{0,1},{8,11},{1,2},{9,8},{2,3},{10,9},{3,0},{11,10},{64,65},{72,75... | collective-permute-start | bytes 3145736 | tf_op jit(solution)/shard_map/ppermute | solution.py:53
  78.7 27.0 %collective-permute-start.26 = (bf16[2,256,1024]{2,1,0:T(8,128)(2,1)S(1)}, bf16[2,256,1024]{2,1,0:T(8,128)(2,1)}, u32[]{:S(2)}, u32[]{:S(2)}) collective-permute-start(bf16[2,256,1024]{2,1,0:T(8,128)(2,1)S(1)} %pad_maximum_fusion.7), channel_id=1, source_target_pairs={{0,1},{8,11},{1,2},{9,8},{2,3},{10,9},{3,0},{11,10},{64,65},{72,75... | collective-permute-start | bytes 3145736 | tf_op jit(solution)/shard_map/ppermute | solution.py:53
  79.3 20.2 %collective-permute-start.21 = (bf16[384,1024]{1,0:T(8,128)(2,1)S(1)}, bf16[384,1024]{1,0:T(8,128)(2,1)S(1)}, u32[]{:S(2)}, u32[]{:S(2)}) collective-permute-start(bf16[384,1024]{1,0:T(8,128)(2,1)S(1)} %collective-permute-done.19), channel_id=1, source_target_pairs={{0,16},{8,56},{1,17},{9,57},{2,18},{10,58},{3,19},{11,59},{64,80},... | collective-permute-start | bytes 2359304 | tf_op jit(solution)/shard_map/ppermute | solution.py:53
  91.1 52.5 %collective-permute-start.6 = (bf16[4,256,1024]{2,1,0:T(8,128)(2,1)S(1)}, bf16[4,256,1024]{2,1,0:T(8,128)(2,1)}, u32[]{:S(2)}, u32[]{:S(2)}) collective-permute-start(bf16[4,256,1024]{2,1,0:T(8,128)(2,1)S(1)} %get-tuple-element.25), channel_id=1, source_target_pairs={{0,4},{8,12},{1,5},{9,13},{2,6},{10,14},{3,7},{11,15},{64,68},{72,... | collective-permute-start | bytes 6291464 | tf_op jit(solution)/shard_map/ppermute | solution.py:53
  105.7 55.1 %collective-permute-start.27 = (bf16[2,256,1024]{2,1,0:T(8,128)(2,1)}, bf16[2,256,1024]{2,1,0:T(8,128)(2,1)}, u32[]{:S(2)}, u32[]{:S(2)}) collective-permute-start(bf16[2,256,1024]{2,1,0:T(8,128)(2,1)} %collective-permute-done.26), channel_id=1, source_target_pairs={{0,1},{8,11},{1,2},{9,8},{2,3},{10,9},{3,0},{11,10},{64,65},{72,75... | collective-permute-start | bytes 3145736 | tf_op jit(solution)/shard_map/ppermute | solution.py:53
  105.7 27.4 %collective-permute-start.14 = (bf16[2,256,1024]{2,1,0:T(8,128)(2,1)S(1)}, bf16[2,256,1024]{2,1,0:T(8,128)(2,1)S(1)}, u32[]{:S(2)}, u32[]{:S(2)}) collective-permute-start(bf16[2,256,1024]{2,1,0:T(8,128)(2,1)S(1)} %collective-permute-done.13), channel_id=1, source_target_pairs={{0,1},{8,11},{1,2},{9,8},{2,3},{10,9},{3,0},{11,10},{64,65},{72,75... | collective-permute-start | bytes 3145736 | tf_op jit(solution)/shard_map/ppermute | solution.py:53
  142.3 25.1 %collective-permute-start.22 = (bf16[2,128,1024]{2,1,0:T(8,128)(2,1)}, bf16[2,128,1024]{2,1,0:T(8,128)(2,1)S(1)}, u32[]{:S(2)}, u32[]{:S(2)}) collective-permute-start(bf16[2,128,1024]{2,1,0:T(8,128)(2,1)} %bitcast.63), channel_id=1, source_target_pairs={{0,16},{8,56},{1,17},{9,57},{2,18},{10,58},{3,19},{11,59},{64,80},... | collective-permute-start | bytes 1572872 | tf_op jit(solution)/shard_map/ppermute | solution.py:53
  151.5 19.6 %collective-permute-start.8 = (bf16[2,128,1024]{2,1,0:T(8,128)(2,1)}, bf16[2,128,1024]{2,1,0:T(8,128)(2,1)}, u32[]{:S(2)}, u32[]{:S(2)}) collective-permute-start(bf16[2,128,1024]{2,1,0:T(8,128)(2,1)} %bitcast.41), channel_id=1, source_target_pairs={{0,16},{8,56},{1,17},{9,57},{2,18},{10,58},{3,19},{11,59},{64,80},... | collective-permute-start | bytes 1572872 | tf_op jit(solution)/shard_map/ppermute | solution.py:53
  160.8 16.2 %collective-permute-start.28 = (bf16[2,256,1024]{2,1,0:T(8,128)(2,1)}, bf16[2,256,1024]{2,1,0:T(8,128)(2,1)S(1)}, u32[]{:S(2)}, u32[]{:S(2)}) collective-permute-start(bf16[2,256,1024]{2,1,0:T(8,128)(2,1)} %collective-permute-done.27), channel_id=1, source_target_pairs={{0,1},{8,11},{1,2},{9,8},{2,3},{10,9},{3,0},{11,10},{64,65},{72,75... | collective-permute-start | bytes 3145736 | tf_op jit(solution)/shard_map/ppermute | solution.py:53
  168.4 22.9 %collective-permute-start.23 = (bf16[2,128,1024]{2,1,0:T(8,128)(2,1)}, bf16[2,128,1024]{2,1,0:T(8,128)(2,1)}, u32[]{:S(2)}, u32[]{:S(2)}) collective-permute-start(bf16[2,128,1024]{2,1,0:T(8,128)(2,1)} %fusion.3), channel_id=1, source_target_pairs={{0,16},{8,56},{1,17},{9,57},{2,18},{10,58},{3,19},{11,59},{64,80},... | collective-permute-start | bytes 1572872 | tf_op jit(solution)/shard_map/ppermute | solution.py:53
  173.1 27.6 %collective-permute-start.9 = (bf16[2,128,1024]{2,1,0:T(8,128)(2,1)}, bf16[2,128,1024]{2,1,0:T(8,128)(2,1)}, u32[]{:S(2)}, u32[]{:S(2)}) collective-permute-start(bf16[2,128,1024]{2,1,0:T(8,128)(2,1)} %fusion.5), channel_id=1, source_target_pairs={{0,16},{8,56},{1,17},{9,57},{2,18},{10,58},{3,19},{11,59},{64,80},... | collective-permute-start | bytes 1572872 | tf_op jit(solution)/shard_map/ppermute | solution.py:53
  191.3 47.2 %collective-permute-start.36 = (f32[8,128,1024]{2,1,0:T(8,128)S(1)}, f32[8,128,1024]{2,1,0:T(8,128)}, u32[]{:S(2)}, u32[]{:S(2)}) collective-permute-start(f32[8,128,1024]{2,1,0:T(8,128)S(1)} %get-tuple-element.39), channel_id=1, source_target_pairs={{0,8},{8,0},{1,9},{9,1},{2,10},{10,2},{3,11},{11,3},{64,72},{72,64... | collective-permute-start | bytes 12582920 | tf_op jit(solution)/shard_map/ppermute | solution.py:53
  192.8 15.4 %collective-permute-start.24 = (bf16[2,128,1024]{2,1,0:T(8,128)(2,1)S(1)}, bf16[2,128,1024]{2,1,0:T(8,128)(2,1)S(1)}, u32[]{:S(2)}, u32[]{:S(2)}) collective-permute-start(bf16[2,128,1024]{2,1,0:T(8,128)(2,1)S(1)} %fusion.2), channel_id=1, source_target_pairs={{0,16},{8,56},{1,17},{9,57},{2,18},{10,58},{3,19},{11,59},{64,80},... | collective-permute-start | bytes 1572872 | tf_op jit(solution)/shard_map/ppermute | solution.py:53
  202.0 17.8 %collective-permute-start.10 = (bf16[2,128,1024]{2,1,0:T(8,128)(2,1)S(1)}, bf16[2,128,1024]{2,1,0:T(8,128)(2,1)S(1)}, u32[]{:S(2)}, u32[]{:S(2)}) collective-permute-start(bf16[2,128,1024]{2,1,0:T(8,128)(2,1)S(1)} %fusion.4), channel_id=1, source_target_pairs={{0,16},{8,56},{1,17},{9,57},{2,18},{10,58},{3,19},{11,59},{64,80},... | collective-permute-start | bytes 1572872 | tf_op jit(solution)/shard_map/ppermute | solution.py:53
  203.2 13.2 %collective-permute-start.29 = (bf16[128,1024]{1,0:T(8,128)(2,1)S(1)}, bf16[128,1024]{1,0:T(8,128)(2,1)S(1)}, u32[]{:S(2)}, u32[]{:S(2)}) collective-permute-start(bf16[128,1024]{1,0:T(8,128)(2,1)S(1)} %get-tuple-element.58), channel_id=1, source_target_pairs={{0,16},{8,56},{1,17},{9,57},{2,18},{10,58},{3,19},{11,59},{64,80},... | collective-permute-start | bytes 786440 | tf_op jit(solution)/shard_map/ppermute | solution.py:53
  208.1 11.2 %collective-permute-start.33 = (bf16[128,1024]{1,0:T(8,128)(2,1)S(1)}, bf16[128,1024]{1,0:T(8,128)(2,1)S(1)}, u32[]{:S(2)}, u32[]{:S(2)}) collective-permute-start(bf16[128,1024]{1,0:T(8,128)(2,1)S(1)} %fusion.12), channel_id=1, source_target_pairs={{0,16},{8,56},{1,17},{9,57},{2,18},{10,58},{3,19},{11,59},{64,80},... | collective-permute-start | bytes 786440 | tf_op jit(solution)/shard_map/ppermute | solution.py:53
  208.4 22.4 %collective-permute-start.25 = (bf16[128,1024]{1,0:T(8,128)(2,1)S(1)}, bf16[128,1024]{1,0:T(8,128)(2,1)S(1)}, u32[]{:S(2)}, u32[]{:S(2)}) collective-permute-start(bf16[128,1024]{1,0:T(8,128)(2,1)S(1)} %fusion.18), channel_id=1, source_target_pairs={{0,64},{8,72},{1,65},{9,73},{2,66},{10,74},{3,67},{11,75},{64,0},{... | collective-permute-start | bytes 786440 | tf_op jit(solution)/shard_map/ppermute | solution.py:53
  220.0 10.9 %collective-permute-start.11 = (bf16[128,1024]{1,0:T(8,128)(2,1)S(1)}, bf16[128,1024]{1,0:T(8,128)(2,1)S(1)}, u32[]{:S(2)}, u32[]{:S(2)}) collective-permute-start(bf16[128,1024]{1,0:T(8,128)(2,1)S(1)} %fusion.17), channel_id=1, source_target_pairs={{0,64},{8,72},{1,65},{9,73},{2,66},{10,74},{3,67},{11,75},{64,0},{... | collective-permute-start | bytes 786440 | tf_op jit(solution)/shard_map/ppermute | solution.py:53
  (22 other events, 179.3 us)

commit v2 on v1

--- a/solution.py
+++ b/solution.py
@@ -165,24 +165,17 @@
     )(order, gate_saved, up_saved, ranks, scales, back_here, back_there)
 
 
-def ring_steps(value, route, tie=()):
-    found = []
-    for step in range(3):
-        value = send(after(value, *tie) if step == 0 and tie else value, route)
-        found.append(value)
-    return found
-
-
 def add(*terms):
     return sum(term.astype(jnp.float32) for term in terms)
 
 
 def reduce_ring(blocks):
-    value = blocks[1]
+    value, first = blocks[1], None
     for step in range(3):
         met = send(value, X_RING)
+        first = met if first is None else first
         if step == 2:
-            return add(met, blocks[0])
+            return add(met, blocks[0]), first
         value = add(met, blocks[step + 2]).astype(jnp.bfloat16)
 
 
@@ -208,34 +201,6 @@
         ]
     ).astype(jnp.int32)
 
-    *own_columns, other_columns = split_columns(out_grad, blocks)
-    met = send(other_columns, CORE)
-    here = [jnp.concatenate([own_columns[chunk], met[chunk]]) for chunk in range(CHUNKS)]
-
-    weight_low = weight[0].astype(jnp.bfloat16)
-    weight_pair = send(weight_low, Y_PAIR)
-    near = [weight_low, *ring_steps(weight_low, X_RING)]
-    far = [weight_pair, *ring_steps(weight_pair, X_RING)]
-
-    first_half = [here[0]]
-    first_half.append(send(here[0], Z_RING))
-    pair_one = send(here[1], Y_HALF)
-    both_one = [after(jnp.stack([here[1], pair_one]), first_half[1])]
-    first_half.append(send(first_half[1], Z_RING))
-    first_half.append(send(first_half[2], Z_RING))
-    both_one += ring_steps(both_one[0], Z_RING)
-    pair_two = send(after(here[2], pair_one), Y_HALF)
-    both_two = [after(jnp.stack([here[2], pair_two]), first_half[3])]
-    both_two += ring_steps(both_two[0], Z_RING)
-    whole_half = jnp.stack(first_half)
-    whole_half = jnp.stack([whole_half, send(after(whole_half, pair_two), Y_HALF)])
-
-    tokens = [
-        whole_half.reshape(EXPERTS * 2 * TOK, WIDE),
-        jnp.stack(both_one, axis=1).reshape(EXPERTS * 2 * TOK, WIDE),
-        jnp.stack(both_two, axis=1).reshape(EXPERTS * 2 * TOK, WIDE),
-    ]
-
     member = jnp.sum(
         (routes[:, :, None] == jnp.arange(EXPERTS, dtype=jnp.int32)).astype(jnp.float32), axis=1
     )
@@ -251,43 +216,92 @@
         axis=1,
     )
     notes = jnp.stack([rank.T, share.T], axis=1).astype(jnp.bfloat16)
-    notes = lax.all_to_all(
-        after(notes, first_half[1]), "expert", split_axis=0, concat_axis=0, tiled=True
-    )
+    notes = lax.all_to_all(notes, "expert", split_axis=0, concat_axis=0, tiled=True)
     ranks, scales = notes[:, 0:1], notes[:, 1:2]
 
     hidden_here = token_hidden(order, gate_saved, up_saved, ranks, scales)
+    *own_columns, other_columns = split_columns(out_grad, blocks)
+    met = send(other_columns, CORE)
+    here = [jnp.concatenate([own_columns[chunk], met[chunk]]) for chunk in range(CHUNKS)]
+
+    weight_low = weight[0].astype(jnp.bfloat16)
+    weight_pair = send(weight_low, Y_PAIR)
+    pair_one = send(here[1], Y_HALF)
+    pair_two = send(here[2], Y_HALF)
+
+    near, far = [weight_low], [weight_pair]
+    first_half = [here[0]]
+    row, column = here[0], weight_low
+    for step in range(3):
+        row, column, hidden_here = lax.optimization_barrier(
+            (send(row, Z_RING), send(column, X_RING), hidden_here)
+        )
+        first_half.append(row)
+        near.append(column)
+    whole_half = jnp.stack(first_half)
+    whole_half = jnp.stack([whole_half, send(after(whole_half, pair_one, pair_two), Y_HALF)])
+
+    both_one = [after(jnp.stack([here[1], pair_one]), row)]
+    row, column = both_one[0], after(weight_pair, column)
+    for step in range(3):
+        row, column = lax.optimization_barrier((send(row, Z_RING), send(column, X_RING)))
+        both_one.append(row)
+        far.append(column)
+    both_two = [after(jnp.stack([here[2], pair_two]), row)]
+    both_two.append(send(both_two[0], Z_RING))
+
+    tokens = [
+        whole_half.reshape(EXPERTS * 2 * TOK, WIDE),
+        jnp.stack(both_one, axis=1).reshape(EXPERTS * 2 * TOK, WIDE),
+    ]
+
     hidden_there = send(hidden_here, CORE)
     mirror = [dy * 4 + (4 - k) % 4 for dy in range(2) for k in range(4)]
     hidden = jnp.stack(
         [hidden_here, jnp.stack([hidden_there[r] for r in mirror])], axis=1
     ).reshape(EXPERTS * 2 * TOK, FF)
 
-    gathered = jnp.stack([w[k] for k in range(4) for w in (near, far)])
-    tokens[1], gathered = lax.optimization_barrier((tokens[1], gathered))
-
-    sums = [None] * CHUNKS
-    for chunk in (1, 0, 2):
+    def weight_term(chunk):
         product = lax.dot_general(
             tokens[chunk], hidden, (((0,), (0,)), ((), ())), preferred_element_type=jnp.float32
         ).astype(jnp.bfloat16)
-        product = product.reshape(4, 2, PART, FF)
-        if chunk == 2:
-            other = reduce_ring([product[k, 1] for k in range(4)]).astype(jnp.bfloat16)
-            mine = reduce_ring([product[k, 0] for k in range(4)])
-        else:
-            mine, other = reduce_ring([product[k] for k in range(4)])
-            other = other.astype(jnp.bfloat16)
-        sums[chunk] = mine + send(other, Y_PAIR).astype(jnp.float32)
-
-    back = sum(
-        jnp.dot(
+        return product.reshape(4, 2, PART, FF)
+
+    def back_term(chunk):
+        return jnp.dot(
             tokens[chunk],
             gathered[:, chunk * PART : (chunk + 1) * PART].reshape(WIDE, FF),
             preferred_element_type=jnp.float32,
         )
-        for chunk in (1, 0, 2)
-    ).reshape(EXPERTS, 2, TOK, FF)
+
+    gathered = jnp.stack([w[k] for k in range(4) for w in (near, far)])
+    product_one = weight_term(1)
+    row, product_one = lax.optimization_barrier((both_two[1], product_one))
+    passed = send(product_one[1], X_RING)
+    row, passed = lax.optimization_barrier((send(row, Z_RING), passed))
+    both_two.append(row)
+    passed = send(add(passed, product_one[2]).astype(jnp.bfloat16), X_RING)
+    row, passed = lax.optimization_barrier((send(row, Z_RING), passed))
+    both_two.append(row)
+    tokens.append(jnp.stack(both_two, axis=1).reshape(EXPERTS * 2 * TOK, WIDE))
+    tokens[0] = after(tokens[0], row)
+    passed = send(add(passed, product_one[3]).astype(jnp.bfloat16), X_RING)
+    mine, other = add(passed, product_one[0])
+
+    sums = [None] * CHUNKS
+    sums[1] = mine + send(other.astype(jnp.bfloat16), Y_PAIR).astype(jnp.float32)
+    product_zero = weight_term(0)
+    (mine, other), met_zero = reduce_ring([product_zero[k] for k in range(4)])
+    sums[0] = mine + send(other.astype(jnp.bfloat16), Y_PAIR).astype(jnp.float32)
+    product_two = weight_term(2)
+    other, met_two = reduce_ring([product_two[k, 1] for k in range(4)])
+    mine, met_last = reduce_ring([product_two[k, 0] for k in range(4)])
+    sums[2] = mine + send(other.astype(jnp.bfloat16), Y_PAIR).astype(jnp.float32)
+
+    back = back_term(1)
+    tokens[0] = after(tokens[0], met_zero, product_two)
+    tokens[2] = after(tokens[2], met_two, met_last)
+    back = (back + back_term(0) + back_term(2)).reshape(EXPERTS, 2, TOK, FF)
     back_there = send(back[:, 1], CORE)
     gate_grad, up_grad, prob_rows = slot_grads(
         order, gate_saved, up_saved, ranks, scales, back[:, 0], back_there

time: 262 us -> 284 us (1.084)
  waiting for transfers between devices: 105 us -> 143 us
  local copies, waits for them, and re-layouts: 22.8 us -> 13.7 us
  other arithmetic: 25.7 us -> 18.4 us
    ppermute x37, waiting for transfers between devices: 101 us -> 133 us  [send(): return lax.ppermute(value, AXES, route)]
    unnamed x43 -> x77, local copies, waits for them, and re-layouts: 11.5 us -> 3.46 us
    all_to_all x1, waiting for transfers between devices: 1.59 us -> 7.01 us  [on_device(): lax.all_to_all(notes, 'expert', split_axis=0, concat_axis=0, tiled=True)]
    convert_element_type x7 -> x5, other arithmetic: 6.09 us -> 0.83 us  [reduce_ring(): value = add(met, blocks[step + 2]).astype(jnp.bfloat16)]
  transfers between devices with their start and end apart: 39 -> 39, of which waited for: 18 -> 24; matrix products, arithmetic and copies ran while one was open for 31% -> 14% of each run, Pallas kernels for 3% -> 3%
where the time goes in v2:
time: 284 us; the launch traced here: 283 us
  waiting for transfers between devices  143 us (50%)
  starting transfers between devices  45.6 us (16%)
  matrix products  36.1 us (13%)
  Pallas kernels  24.7 us (9%)
  other arithmetic  18.4 us (6%)
  local copies, waits for them, and re-layouts  13.7 us (5%)
    ppermute x37, waiting for transfers between devices, send(): return lax.ppermute(value, AXES, route)  133 us
    ppermute x37, starting transfers between devices, send(): return lax.ppermute(value, AXES, route)  32.7 us
    dot_general x3, matrix products, back_term(): jnp.dot(tokens[chunk], gathered[:, chunk * PART:(chunk + 1) * PART].resha...  21.6 us
    dot_general x3, matrix products, weight_term(): lax.dot_general(tokens[chunk], hidden, (((0,), (0,)), ((), ())), preferre...  14.3 us
    pallas_call x1, Pallas kernels, slot_grads(): pl.pallas_call(body, out_shape=(slots, slots, jax.ShapeDtypeStruct((EXPER...  10.5 us
    pallas_call x1, Pallas kernels, token_hidden(): pl.pallas_call(body, out_shape=jax.ShapeDtypeStruct((EXPERTS, TOK, FF), j...  7.83 us
    all_to_all x1, starting transfers between devices, on_device(): lax.all_to_all(notes, 'expert', split_axis=0, concat_axis=0, tiled=True)  7.49 us
    all_to_all x1, waiting for transfers between devices, on_device(): lax.all_to_all(notes, 'expert', split_axis=0, concat_axis=0, tiled=True)  7.01 us
  transfers between devices with their start and end apart: 39, of which 24 were waited for; matrix products, arithmetic and copies ran while one was open for 14% of the time, Pallas kernels for 3%

profile of v2, /device:TPU:0, one launch (start us, length us, event | category | flops | bytes accessed | tf_op | source)
XLA Modules:
  0.0 282.7 jit_solution(4512976825663838481)
XLA Ops:
  1.5 6.4 %split_columns.1 = (bf16[128,1024]{1,0:T(8,128)(2,1)}, bf16[128,1024]{1,0:T(8,128)(2,1)}, bf16[128,1024]{1,0:T(8,128)(2,1)}, bf16[3,128,1024]{2,1,0:T(8,128)(2,1)}) custom-call(s32[16]{0:T(128)} %stack.215.blocks_ref, bf16[128,6144]{1,0:T(8,128)(2,1)} %other_in_ref.1, bf16[128,6144]{1,0:T(8,128)(2,1)} %other_in_ref.1), custom_call_target="tpu_custom_call" | custom-call | tf_op jit(solution)/shard_map/split_columns/pallas_call | solution.py:68
  14.3 7.5 %all-to-all-start = ((bf16[8,2,128]{2,1,0:T(2,128)(2,1)}), bf16[8,2,128]{2,1,0:T(2,128)(2,1)S(1)}, u32[]{:S(2)}, u32[]{:S(2)}) async-start(bf16[8,2,128]{2,1,0:T(2,128)(2,1)} %pad_maximum_fusion.11), calls=%async_computation | async-start | bytes 8192 | tf_op jit(solution)/shard_map/all_to_all | solution.py:219
  22.4 7.0 %all-to-all-done = bf16[8,2,128]{2,1,0:T(2,128)(2,1)S(1)} async-done(((bf16[8,2,128]{2,1,0:T(2,128)(2,1)}), bf16[8,2,128]{2,1,0:T(2,128)(2,1)S(1)}, u32[]{:S(2)}, u32[]{:S(2)}) %all-to-all-start) | async-done | bytes 4128 | tf_op jit(solution)/shard_map/all_to_all | solution.py:219
  30.0 7.8 %token_hidden.1 = bf16[8,128,1024]{2,1,0:T(8,128)(2,1)} custom-call(s32[8]{0:T(128)} %stack.225.order_ref, bf16[768,1024]{1,0:T(8,128)(2,1)} %gate_ref.3, bf16[768,1024]{1,0:T(8,128)(2,1)} %up_ref.3, bf16[8,1,128]{2,1,0:T(2,128)(2,1)} %get-tuple-element.108.rank_ref, bf16[8,1,128]{2,1,0:T(2,128)(2,1)} %get-tuple-element.107.scale_ref), custom_call_target="tpu_custom_call" | custom-call | tf_op jit(solution)/shard_map/token_hidden/pallas_call | solution.py:108
  40.0 10.0 %collective-permute-done.3 = bf16[256,1024]{1,0:T(8,128)(2,1)S(1)} collective-permute-done((bf16[256,1024]{1,0:T(8,128)(2,1)}, bf16[256,1024]{1,0:T(8,128)(2,1)S(1)}, u32[]{:S(2)}, u32[]{:S(2)}) %collective-permute-start.3) | collective-permute-done | bytes 524320 | tf_op jit(solution)/shard_map/ppermute | solution.py:53
  54.4 14.6 %collective-permute-done.7 = bf16[256,1024]{1,0:T(8,128)(2,1)S(1)} collective-permute-done((bf16[256,1024]{1,0:T(8,128)(2,1)S(1)}, bf16[256,1024]{1,0:T(8,128)(2,1)S(1)}, u32[]{:S(2)}, u32[]{:S(2)}) %collective-permute-start.7) | collective-permute-done | bytes 524320 | tf_op jit(solution)/shard_map/ppermute | solution.py:53
  69.7 11.6 %collective-permute-done.11 = bf16[384,1024]{1,0:T(8,128)(2,1)S(1)} collective-permute-done((bf16[384,1024]{1,0:T(8,128)(2,1)}, bf16[384,1024]{1,0:T(8,128)(2,1)S(1)}, u32[]{:S(2)}, u32[]{:S(2)}) %collective-permute-start.11) | collective-permute-done | bytes 786464 | tf_op jit(solution)/shard_map/ppermute | solution.py:53
  81.4 3.7 %collective-permute-start.8 = (bf16[256,1024]{1,0:T(8,128)(2,1)S(1)}, bf16[256,1024]{1,0:T(8,128)(2,1)S(1)}, u32[]{:S(2)}, u32[]{:S(2)}) collective-permute-start(bf16[256,1024]{1,0:T(8,128)(2,1)S(1)} %get-tuple-element.106), channel_id=1, source_target_pairs={{0,4},{8,12},{1,5},{9,13},{2,6},{10,14},{3,7},{11,15},{64,68},{72,... | collective-permute-start | bytes 1572872 | tf_op jit(solution)/shard_map/ppermute | solution.py:53
  85.0 9.4 %collective-permute-done.12 = bf16[384,1024]{1,0:T(8,128)(2,1)S(1)} collective-permute-done((bf16[384,1024]{1,0:T(8,128)(2,1)S(1)}, bf16[384,1024]{1,0:T(8,128)(2,1)S(1)}, u32[]{:S(2)}, u32[]{:S(2)}) %collective-permute-start.12) | collective-permute-done | bytes 786464 | tf_op jit(solution)/shard_map/ppermute | solution.py:53
  97.5 3.6 %collective-permute-start.9 = (bf16[4,256,1024]{2,1,0:T(8,128)(2,1)S(1)}, bf16[4,256,1024]{2,1,0:T(8,128)(2,1)}, u32[]{:S(2)}, u32[]{:S(2)}) collective-permute-start(bf16[4,256,1024]{2,1,0:T(8,128)(2,1)S(1)} %get-tuple-element.52), channel_id=1, source_target_pairs={{0,4},{8,12},{1,5},{9,13},{2,6},{10,14},{3,7},{11,15},{64,68},{72,... | collective-permute-start | bytes 6291464 | tf_op jit(solution)/shard_map/ppermute | solution.py:53
  101.1 7.2 %collective-permute-done.14 = bf16[384,1024]{1,0:T(8,128)(2,1)} collective-permute-done((bf16[384,1024]{1,0:T(8,128)(2,1)S(1)}, bf16[384,1024]{1,0:T(8,128)(2,1)}, u32[]{:S(2)}, u32[]{:S(2)}) %collective-permute-start.14) | collective-permute-done | bytes 786464 | tf_op jit(solution)/shard_map/ppermute | solution.py:53
  111.7 12.2 %collective-permute-done.16 = bf16[384,1024]{1,0:T(8,128)(2,1)S(1)} collective-permute-done((bf16[384,1024]{1,0:T(8,128)(2,1)}, bf16[384,1024]{1,0:T(8,128)(2,1)S(1)}, u32[]{:S(2)}, u32[]{:S(2)}) %collective-permute-start.16) | collective-permute-done | bytes 786464 | tf_op jit(solution)/shard_map/ppermute | solution.py:53
  128.9 4.8 %convolution_convert_fusion.2 = bf16[1024,1024]{1,0:T(8,128)(2,1)S(1)} fusion(bf16[2048,1024]{1,0:T(8,128)(2,1)S(1)} %bitcast.192, bf16[2048,1024]{1,0:T(8,128)(2,1)S(1)} %bitcast.189), kind=kOutput, calls=%fused_computation.10 | convolution fusion | flops 4296015872 | bytes 10485760 | tf_op jit(solution)/shard_map/dot_general | solution.py:265
  133.7 11.2 %collective-permute-done.17 = bf16[2,256,1024]{2,1,0:T(8,128)(2,1)S(1)} collective-permute-done((bf16[2,256,1024]{2,1,0:T(8,128)(2,1)S(1)}, bf16[2,256,1024]{2,1,0:T(8,128)(2,1)S(1)}, u32[]{:S(2)}, u32[]{:S(2)}) %collective-permute-start.17) | collective-permute-done | bytes 1048608 | tf_op jit(solution)/shard_map/ppermute | solution.py:53
  146.5 9.1 %collective-permute-done.20 = bf16[2,128,1024]{2,1,0:T(8,128)(2,1)S(1)} collective-permute-done((bf16[2,128,1024]{2,1,0:T(8,128)(2,1)S(1)}, bf16[2,128,1024]{2,1,0:T(8,128)(2,1)S(1)}, u32[]{:S(2)}, u32[]{:S(2)}) %collective-permute-start.20) | collective-permute-done | bytes 524320 | tf_op jit(solution)/shard_map/ppermute | solution.py:53
  155.6 5.5 %collective-permute-done.19 = bf16[2,256,1024]{2,1,0:T(8,128)(2,1)} collective-permute-done((bf16[2,256,1024]{2,1,0:T(8,128)(2,1)S(1)}, bf16[2,256,1024]{2,1,0:T(8,128)(2,1)}, u32[]{:S(2)}, u32[]{:S(2)}) %collective-permute-start.19) | collective-permute-done | bytes 1048608 | tf_op jit(solution)/shard_map/ppermute | solution.py:53
  164.2 3.2 %fusion.29 = (bf16[8,128,1024]{2,1,0:T(8,128)(2,1)S(1)}, bf16[8,128,1024]{2,1,0:T(8,128)(2,1)}, bf16[8,128,1024]{2,1,0:T(8,128)(2,1)}) fusion(bf16[8,384,1024]{2,1,0:T(8,128)(2,1)S(1)} %bitcast_dynamic-update-slice_fusion), kind=kLoop, calls=%fused_computation.103 | loop fusion | bytes 12582912 | tf_op jit(solution)/shard_map/slice | solution.py:273
  167.4 6.3 %collective-permute-done.22 = bf16[2,128,1024]{2,1,0:T(8,128)(2,1)S(1)} collective-permute-done((bf16[2,128,1024]{2,1,0:T(8,128)(2,1)S(1)}, bf16[2,128,1024]{2,1,0:T(8,128)(2,1)S(1)}, u32[]{:S(2)}, u32[]{:S(2)}) %collective-permute-start.22) | collective-permute-done | bytes 524320 | tf_op jit(solution)/shard_map/ppermute | solution.py:53
  173.7 3.7 %collective-permute-done.21 = bf16[2,256,1024]{2,1,0:T(8,128)(2,1)} collective-permute-done((bf16[2,256,1024]{2,1,0:T(8,128)(2,1)}, bf16[2,256,1024]{2,1,0:T(8,128)(2,1)}, u32[]{:S(2)}, u32[]{:S(2)}) %collective-permute-start.21) | collective-permute-done | bytes 1048608 | tf_op jit(solution)/shard_map/ppermute | solution.py:53
  179.6 4.8 %convolution_convert_fusion = bf16[1024,1024]{1,0:T(8,128)(2,1)S(1)} fusion(bf16[2048,1024]{1,0:T(8,128)(2,1)S(1)} %bitcast.196, bf16[2048,1024]{1,0:T(8,128)(2,1)S(1)} %bitcast.190), kind=kOutput, calls=%fused_computation.8 | convolution fusion | flops 4296015872 | bytes 10485760 | tf_op jit(solution)/shard_map/dot_general | solution.py:265
  185.5 4.8 %convolution_convert_fusion.1 = bf16[1024,1024]{1,0:T(8,128)(2,1)S(1)} fusion(bf16[2048,1024]{1,0:T(8,128)(2,1)S(1)} %bitcast.194, bf16[2048,1024]{1,0:T(8,128)(2,1)S(1)} %bitcast.191), kind=kOutput, calls=%fused_computation.9 | convolution fusion | flops 4296015872 | bytes 10485760 | tf_op jit(solution)/shard_map/dot_general | solution.py:265
  190.6 4.0 %collective-permute-start.23 = (bf16[2,128,1024]{2,1,0:T(8,128)(2,1)S(1)}, bf16[2,128,1024]{2,1,0:T(8,128)(2,1)S(1)}, u32[]{:S(2)}, u32[]{:S(2)}) collective-permute-start(bf16[2,128,1024]{2,1,0:T(8,128)(2,1)S(1)} %bitcast.223), channel_id=1, source_target_pairs={{0,16},{8,56},{1,17},{9,57},{2,18},{10,58},{3,19},{11,59},{64,80},... | collective-permute-start | bytes 1572872 | tf_op jit(solution)/shard_map/ppermute | solution.py:53
  194.6 6.7 %fusion.32 = f32[2048,1024]{1,0:T(8,128)} fusion(bf16[2048,1024]{1,0:T(8,128)(2,1)S(1)} %bitcast.193, bf16[1024,1024]{1,0:T(8,128)(2,1)S(1)} %bitcast.212), kind=kOutput, calls=%fused_computation.106 | convolution fusion | flops 4294967296 | bytes 14680064 | tf_op jit(solution)/shard_map/dot_general | solution.py:271
  201.3 6.7 %fusion.33 = f32[2048,1024]{1,0:T(8,128)} fusion(bf16[2048,1024]{1,0:T(8,128)(2,1)S(1)} %bitcast.195, bf16[1024,1024]{1,0:T(8,128)(2,1)S(1)} %bitcast.211), kind=kOutput, calls=%fused_computation.107 | convolution fusion | flops 4294967296 | bytes 14680064 | tf_op jit(solution)/shard_map/dot_general | solution.py:271
  208.0 8.2 %add_add_fusion = f32[2048,1024]{1,0:T(8,128)S(1)} fusion(f32[2048,1024]{1,0:T(8,128)} %fusion.32, f32[2048,1024]{1,0:T(8,128)} %fusion.33, bf16[2048,1024]{1,0:T(8,128)(2,1)S(1)} %bitcast.197, bf16[1024,1024]{1,0:T(8,128)(2,1)S(1)} %bitcast.210), kind=kOutput, calls=%fused_computation | convolution fusion | flops 4299161600 | bytes 31457280 | tf_op jit(solution)/shard_map/dot_general | solution.py:271
  216.3 3.2 %slice_bitcast_fusion = (f32[8,128,1024]{2,1,0:T(8,128)S(1)}, f32[8,128,1024]{2,1,0:T(8,128)}) fusion(f32[8,2,128,1024]{3,2,1,0:T(8,128)S(1)} %bitcast.187), kind=kLoop, calls=%fused_computation.1 | loop fusion | bytes 16777216 | tf_op jit(solution)/shard_map/squeeze | solution.py:305
  223.8 9.2 %collective-permute-done.33 = bf16[128,1024]{1,0:T(8,128)(2,1)S(1)} collective-permute-done((bf16[128,1024]{1,0:T(8,128)(2,1)S(1)}, bf16[128,1024]{1,0:T(8,128)(2,1)S(1)}, u32[]{:S(2)}, u32[]{:S(2)}) %collective-permute-start.33) | collective-permute-done | bytes 262176 | tf_op jit(solution)/shard_map/ppermute | solution.py:53
  235.0 3.6 %collective-permute-done.27 = bf16[2,128,1024]{2,1,0:T(8,128)(2,1)S(1)} collective-permute-done((bf16[2,128,1024]{2,1,0:T(8,128)(2,1)S(1)}, bf16[2,128,1024]{2,1,0:T(8,128)(2,1)S(1)}, u32[]{:S(2)}, u32[]{:S(2)}) %collective-permute-start.27) | collective-permute-done | bytes 524320 | tf_op jit(solution)/shard_map/ppermute | solution.py:53
  254.1 4.6 %collective-permute-done.26 = bf16[128,1024]{1,0:T(8,128)(2,1)S(1)} collective-permute-done((bf16[128,1024]{1,0:T(8,128)(2,1)S(1)}, bf16[128,1024]{1,0:T(8,128)(2,1)S(1)}, u32[]{:S(2)}, u32[]{:S(2)}) %collective-permute-start.26) | collective-permute-done | bytes 262176 | tf_op jit(solution)/shard_map/ppermute | solution.py:53
  258.8 10.5 %slot_grads.1 = (bf16[768,1024]{1,0:T(8,128)(2,1)}, bf16[768,1024]{1,0:T(8,128)(2,1)}, f32[8,1,128]{2,1,0:T(1,128)}) custom-call(s32[8]{0:T(128)} %stack.225.order_ref, bf16[768,1024]{1,0:T(8,128)(2,1)} %gate_ref.3, bf16[768,1024]{1,0:T(8,128)(2,1)} %up_ref.3, bf16[8,1,128]{2,1,0:T(2,128)(2,1)} %get-tuple-element.108.rank_ref, ...), custom_call_target="tpu_custom_call" | custom-call | tf_op jit(solution)/shard_map/slot_grads/pallas_call | solution.py:155
  269.2 5.4 %all-to-all-start.1 = ((f32[8,1,128]{2,1,0:T(1,128)}), f32[8,1,128]{2,1,0:T(1,128)S(1)}, u32[]{:S(2)}, u32[]{:S(2)}) async-start(f32[8,1,128]{2,1,0:T(1,128)} %get-tuple-element.75), calls=%async_computation.1 | async-start | bytes 8192 | tf_op jit(solution)/shard_map/all_to_all | solution.py:309
  274.6 4.9 %multiply_subtract_fusion = (f32[1,384,1024]{2,1,0:T(8,128)}, f32[1,384,1024]{2,1,0:T(8,128)}, f32[1,384,1024]{2,1,0:T(8,128)}) fusion(f32[1,384,1024]{2,1,0:T(8,128)S(1)} %copy-done, f32[1,128,1024]{2,1,0:T(8,128)S(1)} %fusion.14, f32[1,128,1024]{2,1,0:T(8,128)S(1)} %fusion.7, f32[1,128,1024]{2,1,0:T(8,128)S(1)} %fusion.9, f32[1,384,1024]{2,1,0:T(8,128)} %param.14, ...), kind=kLoop, calls=%fused_computation.12 | loop fusion | flops 7077888 | bytes 11010048 | tf_op jit(solution)/shard_map/sub | solution.py:324
  (181 shorter events, 59.9 us)
Async XLA Ops:
  9.0 28.9 %collective-permute-start.2 = (bf16[384,1024]{1,0:T(8,128)(2,1)}, bf16[384,1024]{1,0:T(8,128)(2,1)S(1)}, u32[]{:S(2)}, u32[]{:S(2)}) collective-permute-start(bf16[384,1024]{1,0:T(8,128)(2,1)} %convert_bitcast_fusion), channel_id=1, source_target_pairs={{0,16},{8,56},{1,17},{9,57},{2,18},{10,58},{3,19},{11,59},{64,80},... | collective-permute-start | bytes 2359304 | tf_op jit(solution)/shard_map/ppermute | solution.py:53
  11.6 26.3 %collective-permute-start.1 = (bf16[256,1024]{1,0:T(8,128)(2,1)}, bf16[256,1024]{1,0:T(8,128)(2,1)}, u32[]{:S(2)}, u32[]{:S(2)}) collective-permute-start(bf16[256,1024]{1,0:T(8,128)(2,1)} %get-tuple-element.102), channel_id=1, source_target_pairs={{0,1},{8,11},{1,2},{9,8},{2,3},{10,9},{3,0},{11,10},{64,65},{72,75... | collective-permute-start | bytes 1572872 | tf_op jit(solution)/shard_map/ppermute | solution.py:53
  14.3 15.1 %all-to-all-start = ((bf16[8,2,128]{2,1,0:T(2,128)(2,1)}), bf16[8,2,128]{2,1,0:T(2,128)(2,1)S(1)}, u32[]{:S(2)}, u32[]{:S(2)}) async-start(bf16[8,2,128]{2,1,0:T(2,128)(2,1)} %pad_maximum_fusion.11), calls=%async_computation | async-start | bytes 8192 | tf_op jit(solution)/shard_map/all_to_all | solution.py:219
  37.9 13.3 %collective-permute-start.4 = (bf16[384,1024]{1,0:T(8,128)(2,1)S(1)}, bf16[384,1024]{1,0:T(8,128)(2,1)S(1)}, u32[]{:S(2)}, u32[]{:S(2)}) collective-permute-start(bf16[384,1024]{1,0:T(8,128)(2,1)S(1)} %collective-permute-done.2), channel_id=1, source_target_pairs={{0,16},{8,56},{1,17},{9,57},{2,18},{10,58},{3,19},{11,59},{64,80},... | collective-permute-start | bytes 2359304 | tf_op jit(solution)/shard_map/ppermute | solution.py:53
  39.4 10.6 %collective-permute-start.3 = (bf16[256,1024]{1,0:T(8,128)(2,1)}, bf16[256,1024]{1,0:T(8,128)(2,1)S(1)}, u32[]{:S(2)}, u32[]{:S(2)}) collective-permute-start(bf16[256,1024]{1,0:T(8,128)(2,1)} %collective-permute-done.1), channel_id=1, source_target_pairs={{0,1},{8,11},{1,2},{9,8},{2,3},{10,9},{3,0},{11,10},{64,65},{72,75... | collective-permute-start | bytes 1572872 | tf_op jit(solution)/shard_map/ppermute | solution.py:53
  51.1 18.0 %collective-permute-start.6 = (bf16[384,1024]{1,0:T(8,128)(2,1)S(1)}, bf16[384,1024]{1,0:T(8,128)(2,1)S(1)}, u32[]{:S(2)}, u32[]{:S(2)}) collective-permute-start(bf16[384,1024]{1,0:T(8,128)(2,1)S(1)} %collective-permute-done.4), channel_id=1, source_target_pairs={{0,16},{8,56},{1,17},{9,57},{2,18},{10,58},{3,19},{11,59},{64,80},... | collective-permute-start | bytes 2359304 | tf_op jit(solution)/shard_map/ppermute | solution.py:53
  52.5 16.4 %collective-permute-start.7 = (bf16[256,1024]{1,0:T(8,128)(2,1)S(1)}, bf16[256,1024]{1,0:T(8,128)(2,1)S(1)}, u32[]{:S(2)}, u32[]{:S(2)}) collective-permute-start(bf16[256,1024]{1,0:T(8,128)(2,1)S(1)} %get-tuple-element.104), channel_id=1, source_target_pairs={{0,4},{8,12},{1,5},{9,13},{2,6},{10,14},{3,7},{11,15},{64,68},{72,... | collective-permute-start | bytes 1572872 | tf_op jit(solution)/shard_map/ppermute | solution.py:53
  53.2 15.9 %collective-permute-start.5 = (bf16[256,1024]{1,0:T(8,128)(2,1)S(1)}, bf16[256,1024]{1,0:T(8,128)(2,1)S(1)}, u32[]{:S(2)}, u32[]{:S(2)}) collective-permute-start(bf16[256,1024]{1,0:T(8,128)(2,1)S(1)} %collective-permute-done.3), channel_id=1, source_target_pairs={{0,1},{8,11},{1,2},{9,8},{2,3},{10,9},{3,0},{11,10},{64,65},{72,75... | collective-permute-start | bytes 1572872 | tf_op jit(solution)/shard_map/ppermute | solution.py:53
  53.7 27.6 %collective-permute-start.11 = (bf16[384,1024]{1,0:T(8,128)(2,1)}, bf16[384,1024]{1,0:T(8,128)(2,1)S(1)}, u32[]{:S(2)}, u32[]{:S(2)}) collective-permute-start(bf16[384,1024]{1,0:T(8,128)(2,1)} %convert_bitcast_fusion), channel_id=1, source_target_pairs={{0,64},{8,72},{1,65},{9,73},{2,66},{10,74},{3,67},{11,75},{64,0},{... | collective-permute-start | bytes 2359304 | tf_op jit(solution)/shard_map/ppermute | solution.py:53
  69.1 25.4 %collective-permute-start.10 = (bf16[2,256,1024]{2,1,0:T(8,128)(2,1)S(1)}, bf16[2,256,1024]{2,1,0:T(8,128)(2,1)S(1)}, u32[]{:S(2)}, u32[]{:S(2)}) collective-permute-start(bf16[2,256,1024]{2,1,0:T(8,128)(2,1)S(1)} %pad_maximum_fusion.7), channel_id=1, source_target_pairs={{0,1},{8,11},{1,2},{9,8},{2,3},{10,9},{3,0},{11,10},{64,65},{72,75... | collective-permute-start | bytes 3145736 | tf_op jit(solution)/shard_map/ppermute | solution.py:53
  69.7 40.8 %collective-permute-start.18 = (bf16[8,128,1024]{2,1,0:T(8,128)(2,1)S(1)}, bf16[8,128,1024]{2,1,0:T(8,128)(2,1)S(1)}, u32[]{:S(2)}, u32[]{:S(2)}) collective-permute-start(bf16[8,128,1024]{2,1,0:T(8,128)(2,1)S(1)} %copy-done.1), channel_id=1, source_target_pairs={{0,8},{8,0},{1,9},{9,1},{2,10},{10,2},{3,11},{11,3},{64,72},{72,64... | collective-permute-start | bytes 6291464 | tf_op jit(solution)/shard_map/ppermute | solution.py:53
  81.3 13.2 %collective-permute-start.12 = (bf16[384,1024]{1,0:T(8,128)(2,1)S(1)}, bf16[384,1024]{1,0:T(8,128)(2,1)S(1)}, u32[]{:S(2)}, u32[]{:S(2)}) collective-permute-start(bf16[384,1024]{1,0:T(8,128)(2,1)S(1)} %collective-permute-done.11), channel_id=1, source_target_pairs={{0,16},{8,56},{1,17},{9,57},{2,18},{10,58},{3,19},{11,59},{64,80},... | collective-permute-start | bytes 2359304 | tf_op jit(solution)/shard_map/ppermute | solution.py:53
  81.4 13.7 %collective-permute-start.8 = (bf16[256,1024]{1,0:T(8,128)(2,1)S(1)}, bf16[256,1024]{1,0:T(8,128)(2,1)S(1)}, u32[]{:S(2)}, u32[]{:S(2)}) collective-permute-start(bf16[256,1024]{1,0:T(8,128)(2,1)S(1)} %get-tuple-element.106), channel_id=1, source_target_pairs={{0,4},{8,12},{1,5},{9,13},{2,6},{10,14},{3,7},{11,15},{64,68},{72,... | collective-permute-start | bytes 1572872 | tf_op jit(solution)/shard_map/ppermute | solution.py:53
  94.5 16.0 %collective-permute-start.13 = (bf16[2,256,1024]{2,1,0:T(8,128)(2,1)S(1)}, bf16[2,256,1024]{2,1,0:T(8,128)(2,1)S(1)}, u32[]{:S(2)}, u32[]{:S(2)}) collective-permute-start(bf16[2,256,1024]{2,1,0:T(8,128)(2,1)S(1)} %collective-permute-done.10), channel_id=1, source_target_pairs={{0,1},{8,11},{1,2},{9,8},{2,3},{10,9},{3,0},{11,10},{64,65},{72,75... | collective-permute-start | bytes 3145736 | tf_op jit(solution)/shard_map/ppermute | solution.py:53
  94.9 13.4 %collective-permute-start.14 = (bf16[384,1024]{1,0:T(8,128)(2,1)S(1)}, bf16[384,1024]{1,0:T(8,128)(2,1)}, u32[]{:S(2)}, u32[]{:S(2)}) collective-permute-start(bf16[384,1024]{1,0:T(8,128)(2,1)S(1)} %collective-permute-done.12), channel_id=1, source_target_pairs={{0,16},{8,56},{1,17},{9,57},{2,18},{10,58},{3,19},{11,59},{64,80},... | collective-permute-start | bytes 2359304 | tf_op jit(solution)/shard_map/ppermute | solution.py:53
  97.5 63.6 %collective-permute-start.9 = (bf16[4,256,1024]{2,1,0:T(8,128)(2,1)S(1)}, bf16[4,256,1024]{2,1,0:T(8,128)(2,1)}, u32[]{:S(2)}, u32[]{:S(2)}) collective-permute-start(bf16[4,256,1024]{2,1,0:T(8,128)(2,1)S(1)} %get-tuple-element.52), channel_id=1, source_target_pairs={{0,4},{8,12},{1,5},{9,13},{2,6},{10,14},{3,7},{11,15},{64,68},{72,... | collective-permute-start | bytes 6291464 | tf_op jit(solution)/shard_map/ppermute | solution.py:53
  110.5 13.4 %collective-permute-start.16 = (bf16[384,1024]{1,0:T(8,128)(2,1)}, bf16[384,1024]{1,0:T(8,128)(2,1)S(1)}, u32[]{:S(2)}, u32[]{:S(2)}) collective-permute-start(bf16[384,1024]{1,0:T(8,128)(2,1)} %collective-permute-done.14), channel_id=1, source_target_pairs={{0,16},{8,56},{1,17},{9,57},{2,18},{10,58},{3,19},{11,59},{64,80},... | collective-permute-start | bytes 2359304 | tf_op jit(solution)/shard_map/ppermute | solution.py:53
  110.5 16.1 %collective-permute-start.15 = (bf16[2,256,1024]{2,1,0:T(8,128)(2,1)S(1)}, bf16[2,256,1024]{2,1,0:T(8,128)(2,1)}, u32[]{:S(2)}, u32[]{:S(2)}) collective-permute-start(bf16[2,256,1024]{2,1,0:T(8,128)(2,1)S(1)} %collective-permute-done.13), channel_id=1, source_target_pairs={{0,1},{8,11},{1,2},{9,8},{2,3},{10,9},{3,0},{11,10},{64,65},{72,75... | collective-permute-start | bytes 3145736 | tf_op jit(solution)/shard_map/ppermute | solution.py:53
  128.7 16.3 %collective-permute-start.17 = (bf16[2,256,1024]{2,1,0:T(8,128)(2,1)S(1)}, bf16[2,256,1024]{2,1,0:T(8,128)(2,1)S(1)}, u32[]{:S(2)}, u32[]{:S(2)}) collective-permute-start(bf16[2,256,1024]{2,1,0:T(8,128)(2,1)S(1)} %pad_maximum_fusion.6), channel_id=1, source_target_pairs={{0,1},{8,11},{1,2},{9,8},{2,3},{10,9},{3,0},{11,10},{64,65},{72,75... | collective-permute-start | bytes 3145736 | tf_op jit(solution)/shard_map/ppermute | solution.py:53
  144.9 16.1 %collective-permute-start.19 = (bf16[2,256,1024]{2,1,0:T(8,128)(2,1)S(1)}, bf16[2,256,1024]{2,1,0:T(8,128)(2,1)}, u32[]{:S(2)}, u32[]{:S(2)}) collective-permute-start(bf16[2,256,1024]{2,1,0:T(8,128)(2,1)S(1)} %collective-permute-done.17), channel_id=1, source_target_pairs={{0,1},{8,11},{1,2},{9,8},{2,3},{10,9},{3,0},{11,10},{64,65},{72,75... | collective-permute-start | bytes 3145736 | tf_op jit(solution)/shard_map/ppermute | solution.py:53
  145.1 10.5 %collective-permute-start.20 = (bf16[2,128,1024]{2,1,0:T(8,128)(2,1)S(1)}, bf16[2,128,1024]{2,1,0:T(8,128)(2,1)S(1)}, u32[]{:S(2)}, u32[]{:S(2)}) collective-permute-start(bf16[2,128,1024]{2,1,0:T(8,128)(2,1)S(1)} %slice_bitcast_fusion.4), channel_id=1, source_target_pairs={{0,16},{8,56},{1,17},{9,57},{2,18},{10,58},{3,19},{11,59},{64,80},... | collective-permute-start | bytes 1572872 | tf_op jit(solution)/shard_map/ppermute | solution.py:53
  161.0 16.3 %collective-permute-start.21 = (bf16[2,256,1024]{2,1,0:T(8,128)(2,1)}, bf16[2,256,1024]{2,1,0:T(8,128)(2,1)}, u32[]{:S(2)}, u32[]{:S(2)}) collective-permute-start(bf16[2,256,1024]{2,1,0:T(8,128)(2,1)} %collective-permute-done.19), channel_id=1, source_target_pairs={{0,1},{8,11},{1,2},{9,8},{2,3},{10,9},{3,0},{11,10},{64,65},{72,75... | collective-permute-start | bytes 3145736 | tf_op jit(solution)/shard_map/ppermute | solution.py:53
  184.5 16.8 %collective-permute-start.29 = (bf16[128,1024]{1,0:T(8,128)(2,1)S(1)}, bf16[128,1024]{1,0:T(8,128)(2,1)S(1)}, u32[]{:S(2)}, u32[]{:S(2)}) collective-permute-start(bf16[128,1024]{1,0:T(8,128)(2,1)S(1)} %get-tuple-element.96), channel_id=1, source_target_pairs={{0,16},{8,56},{1,17},{9,57},{2,18},{10,58},{3,19},{11,59},{64,80},... | collective-permute-start | bytes 786440 | tf_op jit(solution)/shard_map/ppermute | solution.py:53
  184.6 16.7 %collective-permute-start.32 = (bf16[128,1024]{1,0:T(8,128)(2,1)S(1)}, bf16[128,1024]{1,0:T(8,128)(2,1)S(1)}, u32[]{:S(2)}, u32[]{:S(2)}) collective-permute-start(bf16[128,1024]{1,0:T(8,128)(2,1)S(1)} %get-tuple-element.97), channel_id=1, source_target_pairs={{0,16},{8,56},{1,17},{9,57},{2,18},{10,58},{3,19},{11,59},{64,80},... | collective-permute-start | bytes 786440 | tf_op jit(solution)/shard_map/ppermute | solution.py:53
  190.6 10.7 %collective-permute-start.23 = (bf16[2,128,1024]{2,1,0:T(8,128)(2,1)S(1)}, bf16[2,128,1024]{2,1,0:T(8,128)(2,1)S(1)}, u32[]{:S(2)}, u32[]{:S(2)}) collective-permute-start(bf16[2,128,1024]{2,1,0:T(8,128)(2,1)S(1)} %bitcast.223), channel_id=1, source_target_pairs={{0,16},{8,56},{1,17},{9,57},{2,18},{10,58},{3,19},{11,59},{64,80},... | collective-permute-start | bytes 1572872 | tf_op jit(solution)/shard_map/ppermute | solution.py:53
  219.5 39.2 %collective-permute-start.36 = (f32[8,128,1024]{2,1,0:T(8,128)S(1)}, f32[8,128,1024]{2,1,0:T(8,128)}, u32[]{:S(2)}, u32[]{:S(2)}) collective-permute-start(f32[8,128,1024]{2,1,0:T(8,128)S(1)} %get-tuple-element.81), channel_id=1, source_target_pairs={{0,8},{8,0},{1,9},{9,1},{2,10},{10,2},{3,11},{11,3},{64,72},{72,64... | collective-permute-start | bytes 12582920 | tf_op jit(solution)/shard_map/ppermute | solution.py:53
  219.7 14.8 %collective-permute-start.24 = (bf16[2,128,1024]{2,1,0:T(8,128)(2,1)S(1)}, bf16[2,128,1024]{2,1,0:T(8,128)(2,1)S(1)}, u32[]{:S(2)}, u32[]{:S(2)}) collective-permute-start(bf16[2,128,1024]{2,1,0:T(8,128)(2,1)S(1)} %fusion.4), channel_id=1, source_target_pairs={{0,16},{8,56},{1,17},{9,57},{2,18},{10,58},{3,19},{11,59},{64,80},... | collective-permute-start | bytes 1572872 | tf_op jit(solution)/shard_map/ppermute | solution.py:53
  222.3 10.7 %collective-permute-start.33 = (bf16[128,1024]{1,0:T(8,128)(2,1)S(1)}, bf16[128,1024]{1,0:T(8,128)(2,1)S(1)}, u32[]{:S(2)}, u32[]{:S(2)}) collective-permute-start(bf16[128,1024]{1,0:T(8,128)(2,1)S(1)} %fusion.12), channel_id=1, source_target_pairs={{0,16},{8,56},{1,17},{9,57},{2,18},{10,58},{3,19},{11,59},{64,80},... | collective-permute-start | bytes 786440 | tf_op jit(solution)/shard_map/ppermute | solution.py:53
  222.7 16.0 %collective-permute-start.27 = (bf16[2,128,1024]{2,1,0:T(8,128)(2,1)S(1)}, bf16[2,128,1024]{2,1,0:T(8,128)(2,1)S(1)}, u32[]{:S(2)}, u32[]{:S(2)}) collective-permute-start(bf16[2,128,1024]{2,1,0:T(8,128)(2,1)S(1)} %fusion.2), channel_id=1, source_target_pairs={{0,16},{8,56},{1,17},{9,57},{2,18},{10,58},{3,19},{11,59},{64,80},... | collective-permute-start | bytes 1572872 | tf_op jit(solution)/shard_map/ppermute | solution.py:53
  234.8 15.1 %collective-permute-start.25 = (bf16[2,128,1024]{2,1,0:T(8,128)(2,1)S(1)}, bf16[2,128,1024]{2,1,0:T(8,128)(2,1)S(1)}, u32[]{:S(2)}, u32[]{:S(2)}) collective-permute-start(bf16[2,128,1024]{2,1,0:T(8,128)(2,1)S(1)} %fusion.3), channel_id=1, source_target_pairs={{0,16},{8,56},{1,17},{9,57},{2,18},{10,58},{3,19},{11,59},{64,80},... | collective-permute-start | bytes 1572872 | tf_op jit(solution)/shard_map/ppermute | solution.py:53
  238.8 12.9 %collective-permute-start.28 = (bf16[128,1024]{1,0:T(8,128)(2,1)S(1)}, bf16[128,1024]{1,0:T(8,128)(2,1)S(1)}, u32[]{:S(2)}, u32[]{:S(2)}) collective-permute-start(bf16[128,1024]{1,0:T(8,128)(2,1)S(1)} %fusion.18), channel_id=1, source_target_pairs={{0,64},{8,72},{1,65},{9,73},{2,66},{10,74},{3,67},{11,75},{64,0},{... | collective-permute-start | bytes 786440 | tf_op jit(solution)/shard_map/ppermute | solution.py:53
  269.2 12.9 %all-to-all-start.1 = ((f32[8,1,128]{2,1,0:T(1,128)}), f32[8,1,128]{2,1,0:T(1,128)S(1)}, u32[]{:S(2)}, u32[]{:S(2)}) async-start(f32[8,1,128]{2,1,0:T(1,128)} %get-tuple-element.75), calls=%async_computation.1 | async-start | bytes 8192 | tf_op jit(solution)/shard_map/all_to_all | solution.py:309
  (39 other events, 414.9 us)

commit v3 on v1

--- a/solution.py
+++ b/solution.py
@@ -178,11 +178,12 @@
 
 
 def reduce_ring(blocks):
-    value = blocks[1]
+    value, first = blocks[1], None
     for step in range(3):
         met = send(value, X_RING)
+        first = met if first is None else first
         if step == 2:
-            return add(met, blocks[0])
+            return add(met, blocks[0]), first
         value = add(met, blocks[step + 2]).astype(jnp.bfloat16)
 
 
@@ -273,10 +274,13 @@
         ).astype(jnp.bfloat16)
         product = product.reshape(4, 2, PART, FF)
         if chunk == 2:
-            other = reduce_ring([product[k, 1] for k in range(4)]).astype(jnp.bfloat16)
-            mine = reduce_ring([product[k, 0] for k in range(4)])
+            other, met_two = reduce_ring([product[k, 1] for k in range(4)])
+            mine, _ = reduce_ring([product[k, 0] for k in range(4)])
+            other = other.astype(jnp.bfloat16)
+            tokens[1] = after(tokens[1], product)
+            tokens[0], tokens[2] = (after(tokens[c], met_two) for c in (0, 2))
         else:
-            mine, other = reduce_ring([product[k] for k in range(4)])
+            (mine, other), _ = reduce_ring([product[k] for k in range(4)])
             other = other.astype(jnp.bfloat16)
         sums[chunk] = mine + send(other, Y_PAIR).astype(jnp.float32)
 

time: 262 us -> 275 us (1.050)
  waiting for transfers between devices: 105 us -> 126 us
  other arithmetic: 25.7 us -> 19.1 us
    ppermute x37, waiting for transfers between devices: 101 us -> 122 us  [send(): return lax.ppermute(value, AXES, route)]
    convert_element_type x7, other arithmetic: 6.09 us -> 1.22 us  [reduce_ring(): value = add(met, blocks[step + 2]).astype(jnp.bfloat16)]
    unnamed x43 -> x45, local copies, waits for them, and re-layouts: 11.5 us -> 10 us
  transfers between devices with their start and end apart: 39 -> 39, of which waited for: 18 -> 22; matrix products, arithmetic and copies ran while one was open for 31% -> 27% of each run, Pallas kernels for 3% -> 3%
where the time goes in v3:
time: 275 us; the launch traced here: 274 us
  waiting for transfers between devices  126 us (46%)
  starting transfers between devices  45.5 us (17%)
  matrix products  37.1 us (13%)
  Pallas kernels  24.7 us (9%)
  local copies, waits for them, and re-layouts  20.6 us (7%)
  other arithmetic  19.1 us (7%)
    ppermute x37, waiting for transfers between devices, send(): return lax.ppermute(value, AXES, route)  122 us
    ppermute x37, starting transfers between devices, send(): return lax.ppermute(value, AXES, route)  34.3 us
    dot_general x3, matrix products, on_device(): jnp.dot(tokens[chunk], gathered[:, chunk * PART:(chunk + 1) * PART].resha...  21.5 us
    dot_general x3, matrix products, on_device(): lax.dot_general(tokens[chunk], hidden, (((0,), (0,)), ((), ())), preferre...  15.4 us
    pallas_call x1, Pallas kernels, slot_grads(): pl.pallas_call(body, out_shape=(slots, slots, jax.ShapeDtypeStruct((EXPER...  10.5 us
    unnamed x45, local copies, waits for them, and re-layouts  10 us
    all_to_all x1, starting transfers between devices, on_device(): lax.all_to_all(after(notes, first_half[1]), 'expert', split_axis=0, conca...  7.94 us
    pallas_call x1, Pallas kernels, token_hidden(): pl.pallas_call(body, out_shape=jax.ShapeDtypeStruct((EXPERTS, TOK, FF), j...  7.79 us
  transfers between devices with their start and end apart: 39, of which 22 were waited for; matrix products, arithmetic and copies ran while one was open for 27% of the time, Pallas kernels for 3%

profile of v3, /device:TPU:0, one launch (start us, length us, event | category | flops | bytes accessed | tf_op | source)
XLA Modules:
  0.0 274.4 jit_solution(13267709241400784379)
XLA Ops:
  1.4 6.4 %split_columns.1 = (bf16[128,1024]{1,0:T(8,128)(2,1)}, bf16[128,1024]{1,0:T(8,128)(2,1)}, bf16[128,1024]{1,0:T(8,128)(2,1)}, bf16[3,128,1024]{2,1,0:T(8,128)(2,1)}) custom-call(s32[16]{0:T(128)} %stack.215.blocks_ref, bf16[128,6144]{1,0:T(8,128)(2,1)} %other_in_ref.1, bf16[128,6144]{1,0:T(8,128)(2,1)} %other_in_ref.1), custom_call_target="tpu_custom_call" | custom-call | tf_op jit(solution)/shard_map/split_columns/pallas_call | solution.py:68
  12.3 2.9 %collective-permute-start.4 = (bf16[256,1024]{1,0:T(8,128)(2,1)S(1)}, bf16[256,1024]{1,0:T(8,128)(2,1)}, u32[]{:S(2)}, u32[]{:S(2)}) collective-permute-start(bf16[256,1024]{1,0:T(8,128)(2,1)S(1)} %get-tuple-element.72), channel_id=1, source_target_pairs={{0,4},{8,12},{1,5},{9,13},{2,6},{10,14},{3,7},{11,15},{64,68},{72,... | collective-permute-start | bytes 1572872 | tf_op jit(solution)/shard_map/ppermute | solution.py:53
  19.0 9.5 %collective-permute-done.15 = bf16[384,1024]{1,0:T(8,128)(2,1)} collective-permute-done((bf16[384,1024]{1,0:T(8,128)(2,1)S(1)}, bf16[384,1024]{1,0:T(8,128)(2,1)}, u32[]{:S(2)}, u32[]{:S(2)}) %collective-permute-start.15) | collective-permute-done | bytes 786464 | tf_op jit(solution)/shard_map/ppermute | solution.py:53
  33.2 7.9 %all-to-all-start = ((bf16[8,2,128]{2,1,0:T(2,128)(2,1)}), bf16[8,2,128]{2,1,0:T(2,128)(2,1)S(1)}, u32[]{:S(2)}, u32[]{:S(2)}) async-start(bf16[8,2,128]{2,1,0:T(2,128)(2,1)} %pad_maximum_fusion.11), calls=%async_computation | async-start | bytes 8192 | tf_op jit(solution)/shard_map/all_to_all | solution.py:255
  49.3 7.8 %token_hidden.1 = bf16[8,128,1024]{2,1,0:T(8,128)(2,1)} custom-call(s32[8]{0:T(128)} %stack.232.order_ref, bf16[768,1024]{1,0:T(8,128)(2,1)} %gate_ref.3, bf16[768,1024]{1,0:T(8,128)(2,1)} %up_ref.3, bf16[8,1,128]{2,1,0:T(2,128)(2,1)} %get-tuple-element.76.rank_ref, bf16[8,1,128]{2,1,0:T(2,128)(2,1)} %get-tuple-element.75.scale_ref), custom_call_target="tpu_custom_call" | custom-call | tf_op jit(solution)/shard_map/token_hidden/pallas_call | solution.py:108
  62.1 3.7 %collective-permute-done.2 = bf16[256,1024]{1,0:T(8,128)(2,1)} collective-permute-done((bf16[256,1024]{1,0:T(8,128)(2,1)}, bf16[256,1024]{1,0:T(8,128)(2,1)}, u32[]{:S(2)}, u32[]{:S(2)}) %collective-permute-start.2) | collective-permute-done | bytes 524320 | tf_op jit(solution)/shard_map/ppermute | solution.py:53
  70.0 7.7 %collective-permute-done.5 = bf16[256,1024]{1,0:T(8,128)(2,1)S(1)} collective-permute-done((bf16[256,1024]{1,0:T(8,128)(2,1)S(1)}, bf16[256,1024]{1,0:T(8,128)(2,1)S(1)}, u32[]{:S(2)}, u32[]{:S(2)}) %collective-permute-start.5) | collective-permute-done | bytes 524320 | tf_op jit(solution)/shard_map/ppermute | solution.py:53
  85.5 5.5 %collective-permute-done.20 = bf16[384,1024]{1,0:T(8,128)(2,1)S(1)} collective-permute-done((bf16[384,1024]{1,0:T(8,128)(2,1)}, bf16[384,1024]{1,0:T(8,128)(2,1)S(1)}, u32[]{:S(2)}, u32[]{:S(2)}) %collective-permute-start.20) | collective-permute-done | bytes 786464 | tf_op jit(solution)/shard_map/ppermute | solution.py:53
  91.7 7.8 %collective-permute-done.21 = bf16[384,1024]{1,0:T(8,128)(2,1)S(1)} collective-permute-done((bf16[384,1024]{1,0:T(8,128)(2,1)S(1)}, bf16[384,1024]{1,0:T(8,128)(2,1)S(1)}, u32[]{:S(2)}, u32[]{:S(2)}) %collective-permute-start.21) | collective-permute-done | bytes 786464 | tf_op jit(solution)/shard_map/ppermute | solution.py:53
  99.5 6.1 %collective-permute-done.26 = bf16[2,256,1024]{2,1,0:T(8,128)(2,1)} collective-permute-done((bf16[2,256,1024]{2,1,0:T(8,128)(2,1)S(1)}, bf16[2,256,1024]{2,1,0:T(8,128)(2,1)}, u32[]{:S(2)}, u32[]{:S(2)}) %collective-permute-start.26) | collective-permute-done | bytes 1048608 | tf_op jit(solution)/shard_map/ppermute | solution.py:53
  106.9 26.2 %collective-permute-done.14 = bf16[2,256,1024]{2,1,0:T(8,128)(2,1)S(1)} collective-permute-done((bf16[2,256,1024]{2,1,0:T(8,128)(2,1)S(1)}, bf16[2,256,1024]{2,1,0:T(8,128)(2,1)S(1)}, u32[]{:S(2)}, u32[]{:S(2)}) %collective-permute-start.14) | collective-permute-done | bytes 1048608 | tf_op jit(solution)/shard_map/ppermute | solution.py:53
  135.2 4.8 %convolution_convert_fusion.1 = bf16[1024,1024]{1,0:T(8,128)(2,1)S(1)} fusion(bf16[2048,1024]{1,0:T(8,128)(2,1)S(1)} %bitcast.187, bf16[2048,1024]{1,0:T(8,128)(2,1)S(1)} %bitcast.184), kind=kOutput, calls=%fused_computation.9 | convolution fusion | flops 4296015872 | bytes 10485760 | tf_op jit(solution)/shard_map/dot_general | solution.py:272
  145.2 5.8 %convolution_convert_fusion.2 = bf16[1024,1024]{1,0:T(8,128)(2,1)} fusion(bf16[2048,1024]{1,0:T(8,128)(2,1)S(1)} %bitcast.189, bf16[2048,1024]{1,0:T(8,128)(2,1)S(1)} %bitcast.185), kind=kOutput, calls=%fused_computation.10 | convolution fusion | flops 4296015872 | bytes 10485760 | tf_op jit(solution)/shard_map/dot_general | solution.py:272
  151.0 10.4 %collective-permute-done.28 = bf16[2,256,1024]{2,1,0:T(8,128)(2,1)S(1)} collective-permute-done((bf16[2,256,1024]{2,1,0:T(8,128)(2,1)}, bf16[2,256,1024]{2,1,0:T(8,128)(2,1)S(1)}, u32[]{:S(2)}, u32[]{:S(2)}) %collective-permute-start.28) | collective-permute-done | bytes 1048608 | tf_op jit(solution)/shard_map/ppermute | solution.py:53
  163.6 4.8 %convolution_convert_fusion = bf16[1024,1024]{1,0:T(8,128)(2,1)S(1)} fusion(bf16[2048,1024]{1,0:T(8,128)(2,1)S(1)} %bitcast.191, bf16[2048,1024]{1,0:T(8,128)(2,1)S(1)} %bitcast.186), kind=kOutput, calls=%fused_computation.8 | convolution fusion | flops 4296015872 | bytes 10485760 | tf_op jit(solution)/shard_map/dot_general | solution.py:272
  169.3 6.7 %fusion.33 = f32[2048,1024]{1,0:T(8,128)} fusion(bf16[2048,1024]{1,0:T(8,128)(2,1)S(1)} %bitcast.188, bf16[1024,1024]{1,0:T(8,128)(2,1)S(1)} %bitcast.204), kind=kOutput, calls=%fused_computation.106 | convolution fusion | flops 4294967296 | bytes 14680064 | tf_op jit(solution)/shard_map/dot_general | solution.py:288
  176.4 6.6 %fusion.34 = f32[2048,1024]{1,0:T(8,128)} fusion(bf16[2048,1024]{1,0:T(8,128)(2,1)S(1)} %bitcast.190, bf16[1024,1024]{1,0:T(8,128)(2,1)S(1)} %bitcast.203), kind=kOutput, calls=%fused_computation.107 | convolution fusion | flops 4294967296 | bytes 14680064 | tf_op jit(solution)/shard_map/dot_general | solution.py:288
  183.0 8.2 %add_add_fusion = f32[2048,1024]{1,0:T(8,128)S(1)} fusion(f32[2048,1024]{1,0:T(8,128)} %fusion.33, f32[2048,1024]{1,0:T(8,128)} %fusion.34, bf16[2048,1024]{1,0:T(8,128)(2,1)S(1)} %bitcast.192, bf16[1024,1024]{1,0:T(8,128)(2,1)S(1)} %bitcast.202), kind=kOutput, calls=%fused_computation | convolution fusion | flops 4299161600 | bytes 31457280 | tf_op jit(solution)/shard_map/dot_general | solution.py:288
  191.2 3.2 %slice_bitcast_fusion = (f32[8,128,1024]{2,1,0:T(8,128)S(1)}, f32[8,128,1024]{2,1,0:T(8,128)}) fusion(f32[8,2,128,1024]{3,2,1,0:T(8,128)S(1)} %bitcast.182), kind=kLoop, calls=%fused_computation.1 | loop fusion | bytes 16777216 | tf_op jit(solution)/shard_map/squeeze | solution.py:295
  198.0 7.1 %collective-permute-done.8 = bf16[2,128,1024]{2,1,0:T(8,128)(2,1)S(1)} collective-permute-done((bf16[2,128,1024]{2,1,0:T(8,128)(2,1)S(1)}, bf16[2,128,1024]{2,1,0:T(8,128)(2,1)S(1)}, u32[]{:S(2)}, u32[]{:S(2)}) %collective-permute-start.8) | collective-permute-done | bytes 524320 | tf_op jit(solution)/shard_map/ppermute | solution.py:53
  206.4 4.3 %collective-permute-done.23 = bf16[2,128,1024]{2,1,0:T(8,128)(2,1)S(1)} collective-permute-done((bf16[2,128,1024]{2,1,0:T(8,128)(2,1)S(1)}, bf16[2,128,1024]{2,1,0:T(8,128)(2,1)S(1)}, u32[]{:S(2)}, u32[]{:S(2)}) %collective-permute-start.23) | collective-permute-done | bytes 524320 | tf_op jit(solution)/shard_map/ppermute | solution.py:53
  212.0 4.3 %collective-permute-done.9 = bf16[2,128,1024]{2,1,0:T(8,128)(2,1)S(1)} collective-permute-done((bf16[2,128,1024]{2,1,0:T(8,128)(2,1)S(1)}, bf16[2,128,1024]{2,1,0:T(8,128)(2,1)S(1)}, u32[]{:S(2)}, u32[]{:S(2)}) %collective-permute-start.9) | collective-permute-done | bytes 524320 | tf_op jit(solution)/shard_map/ppermute | solution.py:53
  219.3 2.7 collective-permute-done.24
  222.9 7.4 %collective-permute-done.29 = bf16[128,1024]{1,0:T(8,128)(2,1)S(1)} collective-permute-done((bf16[128,1024]{1,0:T(8,128)(2,1)S(1)}, bf16[128,1024]{1,0:T(8,128)(2,1)S(1)}, u32[]{:S(2)}, u32[]{:S(2)}) %collective-permute-start.29) | collective-permute-done | bytes 262176 | tf_op jit(solution)/shard_map/ppermute | solution.py:53
  230.4 2.8 %collective-permute-done.33 = bf16[128,1024]{1,0:T(8,128)(2,1)S(1)} collective-permute-done((bf16[128,1024]{1,0:T(8,128)(2,1)S(1)}, bf16[128,1024]{1,0:T(8,128)(2,1)S(1)}, u32[]{:S(2)}, u32[]{:S(2)}) %collective-permute-start.33) | collective-permute-done | bytes 262176 | tf_op jit(solution)/shard_map/ppermute | solution.py:53
  236.0 5.0 %collective-permute-done.30 = bf16[128,1024]{1,0:T(8,128)(2,1)S(1)} collective-permute-done((bf16[128,1024]{1,0:T(8,128)(2,1)S(1)}, bf16[128,1024]{1,0:T(8,128)(2,1)S(1)}, u32[]{:S(2)}, u32[]{:S(2)}) %collective-permute-start.30) | collective-permute-done | bytes 262176 | tf_op jit(solution)/shard_map/ppermute | solution.py:53
  241.0 2.8 %collective-permute-done.34 = bf16[128,1024]{1,0:T(8,128)(2,1)S(1)} collective-permute-done((bf16[128,1024]{1,0:T(8,128)(2,1)S(1)}, bf16[128,1024]{1,0:T(8,128)(2,1)S(1)}, u32[]{:S(2)}, u32[]{:S(2)}) %collective-permute-start.34) | collective-permute-done | bytes 262176 | tf_op jit(solution)/shard_map/ppermute | solution.py:53
  244.9 5.5 %collective-permute-done.35 = bf16[128,1024]{1,0:T(8,128)(2,1)S(1)} collective-permute-done((bf16[128,1024]{1,0:T(8,128)(2,1)S(1)}, bf16[128,1024]{1,0:T(8,128)(2,1)S(1)}, u32[]{:S(2)}, u32[]{:S(2)}) %collective-permute-start.35) | collective-permute-done | bytes 262176 | tf_op jit(solution)/shard_map/ppermute | solution.py:53
  252.5 10.5 %slot_grads.1 = (bf16[768,1024]{1,0:T(8,128)(2,1)}, bf16[768,1024]{1,0:T(8,128)(2,1)}, f32[8,1,128]{2,1,0:T(1,128)}) custom-call(s32[8]{0:T(128)} %stack.232.order_ref, bf16[768,1024]{1,0:T(8,128)(2,1)} %gate_ref.3, bf16[768,1024]{1,0:T(8,128)(2,1)} %up_ref.3, bf16[8,1,128]{2,1,0:T(2,128)(2,1)} %get-tuple-element.76.rank_ref, ...), custom_call_target="tpu_custom_call" | custom-call | tf_op jit(solution)/shard_map/slot_grads/pallas_call | solution.py:155
  263.0 3.3 %all-to-all-start.1 = ((f32[8,1,128]{2,1,0:T(1,128)}), f32[8,1,128]{2,1,0:T(1,128)S(1)}, u32[]{:S(2)}, u32[]{:S(2)}) async-start(f32[8,1,128]{2,1,0:T(1,128)} %get-tuple-element.39), calls=%async_computation.1 | async-start | bytes 8192 | tf_op jit(solution)/shard_map/all_to_all | solution.py:299
  266.3 4.9 %multiply_subtract_fusion = (f32[1,384,1024]{2,1,0:T(8,128)}, f32[1,384,1024]{2,1,0:T(8,128)}, f32[1,384,1024]{2,1,0:T(8,128)}) fusion(f32[1,384,1024]{2,1,0:T(8,128)S(1)} %copy-done, f32[1,128,1024]{2,1,0:T(8,128)S(1)} %fusion.14, f32[1,128,1024]{2,1,0:T(8,128)S(1)} %fusion.7, f32[1,128,1024]{2,1,0:T(8,128)S(1)} %fusion.9, f32[1,384,1024]{2,1,0:T(8,128)} %param.14, ...), kind=kLoop, calls=%fused_computation.12 | loop fusion | flops 7077888 | bytes 11010048 | tf_op jit(solution)/shard_map/sub | solution.py:314
  271.3 2.5 all-to-all-done.1
  (149 shorter events, 67.8 us)
Async XLA Ops:
  8.0 20.5 %collective-permute-start.15 = (bf16[384,1024]{1,0:T(8,128)(2,1)S(1)}, bf16[384,1024]{1,0:T(8,128)(2,1)}, u32[]{:S(2)}, u32[]{:S(2)}) collective-permute-start(bf16[384,1024]{1,0:T(8,128)(2,1)S(1)} %convert_bitcast_fusion), channel_id=1, source_target_pairs={{0,64},{8,72},{1,65},{9,73},{2,66},{10,74},{3,67},{11,75},{64,0},{... | collective-permute-start | bytes 2359304 | tf_op jit(solution)/shard_map/ppermute | solution.py:53
  9.8 20.6 %collective-permute-start.16 = (bf16[384,1024]{1,0:T(8,128)(2,1)S(1)}, bf16[384,1024]{1,0:T(8,128)(2,1)}, u32[]{:S(2)}, u32[]{:S(2)}) collective-permute-start(bf16[384,1024]{1,0:T(8,128)(2,1)S(1)} %convert_bitcast_fusion), channel_id=1, source_target_pairs={{0,16},{8,56},{1,17},{9,57},{2,18},{10,58},{3,19},{11,59},{64,80},... | collective-permute-start | bytes 2359304 | tf_op jit(solution)/shard_map/ppermute | solution.py:53
  12.3 29.6 %collective-permute-start.4 = (bf16[256,1024]{1,0:T(8,128)(2,1)S(1)}, bf16[256,1024]{1,0:T(8,128)(2,1)}, u32[]{:S(2)}, u32[]{:S(2)}) collective-permute-start(bf16[256,1024]{1,0:T(8,128)(2,1)S(1)} %get-tuple-element.72), channel_id=1, source_target_pairs={{0,4},{8,12},{1,5},{9,13},{2,6},{10,14},{3,7},{11,15},{64,68},{72,... | collective-permute-start | bytes 1572872 | tf_op jit(solution)/shard_map/ppermute | solution.py:53
  16.1 17.1 %collective-permute-start.1 = (bf16[256,1024]{1,0:T(8,128)(2,1)}, bf16[256,1024]{1,0:T(8,128)(2,1)S(1)}, u32[]{:S(2)}, u32[]{:S(2)}) collective-permute-start(bf16[256,1024]{1,0:T(8,128)(2,1)} %get-tuple-element.70), channel_id=1, source_target_pairs={{0,1},{8,11},{1,2},{9,8},{2,3},{10,9},{3,0},{11,10},{64,65},{72,75... | collective-permute-start | bytes 1572872 | tf_op jit(solution)/shard_map/ppermute | solution.py:53
  28.5 30.6 %collective-permute-start.17 = (bf16[384,1024]{1,0:T(8,128)(2,1)}, bf16[384,1024]{1,0:T(8,128)(2,1)}, u32[]{:S(2)}, u32[]{:S(2)}) collective-permute-start(bf16[384,1024]{1,0:T(8,128)(2,1)} %collective-permute-done.15), channel_id=1, source_target_pairs={{0,16},{8,56},{1,17},{9,57},{2,18},{10,58},{3,19},{11,59},{64,80},... | collective-permute-start | bytes 2359304 | tf_op jit(solution)/shard_map/ppermute | solution.py:53
  30.4 31.1 %collective-permute-start.18 = (bf16[384,1024]{1,0:T(8,128)(2,1)}, bf16[384,1024]{1,0:T(8,128)(2,1)}, u32[]{:S(2)}, u32[]{:S(2)}) collective-permute-start(bf16[384,1024]{1,0:T(8,128)(2,1)} %collective-permute-done.16), channel_id=1, source_target_pairs={{0,16},{8,56},{1,17},{9,57},{2,18},{10,58},{3,19},{11,59},{64,80},... | collective-permute-start | bytes 2359304 | tf_op jit(solution)/shard_map/ppermute | solution.py:53
  33.2 15.5 %all-to-all-start = ((bf16[8,2,128]{2,1,0:T(2,128)(2,1)}), bf16[8,2,128]{2,1,0:T(2,128)(2,1)S(1)}, u32[]{:S(2)}, u32[]{:S(2)}) async-start(bf16[8,2,128]{2,1,0:T(2,128)(2,1)} %pad_maximum_fusion.11), calls=%async_computation | async-start | bytes 8192 | tf_op jit(solution)/shard_map/all_to_all | solution.py:255
  43.2 34.8 %collective-permute-start.12 = (bf16[2,256,1024]{2,1,0:T(8,128)(2,1)S(1)}, bf16[2,256,1024]{2,1,0:T(8,128)(2,1)}, u32[]{:S(2)}, u32[]{:S(2)}) collective-permute-start(bf16[2,256,1024]{2,1,0:T(8,128)(2,1)S(1)} %pad_maximum_fusion.6), channel_id=1, source_target_pairs={{0,1},{8,11},{1,2},{9,8},{2,3},{10,9},{3,0},{11,10},{64,65},{72,75... | collective-permute-start | bytes 3145736 | tf_op jit(solution)/shard_map/ppermute | solution.py:53
  45.2 20.6 %collective-permute-start.2 = (bf16[256,1024]{1,0:T(8,128)(2,1)}, bf16[256,1024]{1,0:T(8,128)(2,1)}, u32[]{:S(2)}, u32[]{:S(2)}) collective-permute-start(bf16[256,1024]{1,0:T(8,128)(2,1)} %copy-done.10), channel_id=1, source_target_pairs={{0,1},{8,11},{1,2},{9,8},{2,3},{10,9},{3,0},{11,10},{64,65},{72,75... | collective-permute-start | bytes 1572872 | tf_op jit(solution)/shard_map/ppermute | solution.py:53
  57.1 48.6 %collective-permute-start.7 = (bf16[8,128,1024]{2,1,0:T(8,128)(2,1)}, bf16[8,128,1024]{2,1,0:T(8,128)(2,1)S(1)}, u32[]{:S(2)}, u32[]{:S(2)}) collective-permute-start(bf16[8,128,1024]{2,1,0:T(8,128)(2,1)} %token_hidden.1), channel_id=1, source_target_pairs={{0,8},{8,0},{1,9},{9,1},{2,10},{10,2},{3,11},{11,3},{64,72},{72,64... | collective-permute-start | bytes 6291464 | tf_op jit(solution)/shard_map/ppermute | solution.py:53
  59.2 20.1 %collective-permute-start.19 = (bf16[384,1024]{1,0:T(8,128)(2,1)}, bf16[384,1024]{1,0:T(8,128)(2,1)S(1)}, u32[]{:S(2)}, u32[]{:S(2)}) collective-permute-start(bf16[384,1024]{1,0:T(8,128)(2,1)} %collective-permute-done.17), channel_id=1, source_target_pairs={{0,16},{8,56},{1,17},{9,57},{2,18},{10,58},{3,19},{11,59},{64,80},... | collective-permute-start | bytes 2359304 | tf_op jit(solution)/shard_map/ppermute | solution.py:53
  61.5 16.2 %collective-permute-start.5 = (bf16[256,1024]{1,0:T(8,128)(2,1)S(1)}, bf16[256,1024]{1,0:T(8,128)(2,1)S(1)}, u32[]{:S(2)}, u32[]{:S(2)}) collective-permute-start(bf16[256,1024]{1,0:T(8,128)(2,1)S(1)} %get-tuple-element.27), channel_id=1, source_target_pairs={{0,4},{8,12},{1,5},{9,13},{2,6},{10,14},{3,7},{11,15},{64,68},{72,... | collective-permute-start | bytes 1572872 | tf_op jit(solution)/shard_map/ppermute | solution.py:53
  65.8 12.9 %collective-permute-start.3 = (bf16[256,1024]{1,0:T(8,128)(2,1)}, bf16[256,1024]{1,0:T(8,128)(2,1)S(1)}, u32[]{:S(2)}, u32[]{:S(2)}) collective-permute-start(bf16[256,1024]{1,0:T(8,128)(2,1)} %collective-permute-done.2), channel_id=1, source_target_pairs={{0,1},{8,11},{1,2},{9,8},{2,3},{10,9},{3,0},{11,10},{64,65},{72,75... | collective-permute-start | bytes 1572872 | tf_op jit(solution)/shard_map/ppermute | solution.py:53
  77.6 13.4 %collective-permute-start.20 = (bf16[384,1024]{1,0:T(8,128)(2,1)}, bf16[384,1024]{1,0:T(8,128)(2,1)S(1)}, u32[]{:S(2)}, u32[]{:S(2)}) collective-permute-start(bf16[384,1024]{1,0:T(8,128)(2,1)} %collective-permute-done.18), channel_id=1, source_target_pairs={{0,16},{8,56},{1,17},{9,57},{2,18},{10,58},{3,19},{11,59},{64,80},... | collective-permute-start | bytes 2359304 | tf_op jit(solution)/shard_map/ppermute | solution.py:53
  78.0 27.6 %collective-permute-start.13 = (bf16[2,256,1024]{2,1,0:T(8,128)(2,1)}, bf16[2,256,1024]{2,1,0:T(8,128)(2,1)S(1)}, u32[]{:S(2)}, u32[]{:S(2)}) collective-permute-start(bf16[2,256,1024]{2,1,0:T(8,128)(2,1)} %collective-permute-done.12), channel_id=1, source_target_pairs={{0,1},{8,11},{1,2},{9,8},{2,3},{10,9},{3,0},{11,10},{64,65},{72,75... | collective-permute-start | bytes 3145736 | tf_op jit(solution)/shard_map/ppermute | solution.py:53
  78.7 27.0 %collective-permute-start.26 = (bf16[2,256,1024]{2,1,0:T(8,128)(2,1)S(1)}, bf16[2,256,1024]{2,1,0:T(8,128)(2,1)}, u32[]{:S(2)}, u32[]{:S(2)}) collective-permute-start(bf16[2,256,1024]{2,1,0:T(8,128)(2,1)S(1)} %pad_maximum_fusion.7), channel_id=1, source_target_pairs={{0,1},{8,11},{1,2},{9,8},{2,3},{10,9},{3,0},{11,10},{64,65},{72,75... | collective-permute-start | bytes 3145736 | tf_op jit(solution)/shard_map/ppermute | solution.py:53
  79.2 20.2 %collective-permute-start.21 = (bf16[384,1024]{1,0:T(8,128)(2,1)S(1)}, bf16[384,1024]{1,0:T(8,128)(2,1)S(1)}, u32[]{:S(2)}, u32[]{:S(2)}) collective-permute-start(bf16[384,1024]{1,0:T(8,128)(2,1)S(1)} %collective-permute-done.19), channel_id=1, source_target_pairs={{0,16},{8,56},{1,17},{9,57},{2,18},{10,58},{3,19},{11,59},{64,80},... | collective-permute-start | bytes 2359304 | tf_op jit(solution)/shard_map/ppermute | solution.py:53
  91.1 51.3 %collective-permute-start.6 = (bf16[4,256,1024]{2,1,0:T(8,128)(2,1)S(1)}, bf16[4,256,1024]{2,1,0:T(8,128)(2,1)S(1)}, u32[]{:S(2)}, u32[]{:S(2)}) collective-permute-start(bf16[4,256,1024]{2,1,0:T(8,128)(2,1)S(1)} %get-tuple-element.28), channel_id=1, source_target_pairs={{0,4},{8,12},{1,5},{9,13},{2,6},{10,14},{3,7},{11,15},{64,68},{72,... | collective-permute-start | bytes 6291464 | tf_op jit(solution)/shard_map/ppermute | solution.py:53
  105.7 39.5 %collective-permute-start.27 = (bf16[2,256,1024]{2,1,0:T(8,128)(2,1)}, bf16[2,256,1024]{2,1,0:T(8,128)(2,1)}, u32[]{:S(2)}, u32[]{:S(2)}) collective-permute-start(bf16[2,256,1024]{2,1,0:T(8,128)(2,1)} %collective-permute-done.26), channel_id=1, source_target_pairs={{0,1},{8,11},{1,2},{9,8},{2,3},{10,9},{3,0},{11,10},{64,65},{72,75... | collective-permute-start | bytes 3145736 | tf_op jit(solution)/shard_map/ppermute | solution.py:53
  105.7 27.4 %collective-permute-start.14 = (bf16[2,256,1024]{2,1,0:T(8,128)(2,1)S(1)}, bf16[2,256,1024]{2,1,0:T(8,128)(2,1)S(1)}, u32[]{:S(2)}, u32[]{:S(2)}) collective-permute-start(bf16[2,256,1024]{2,1,0:T(8,128)(2,1)S(1)} %collective-permute-done.13), channel_id=1, source_target_pairs={{0,1},{8,11},{1,2},{9,8},{2,3},{10,9},{3,0},{11,10},{64,65},{72,75... | collective-permute-start | bytes 3145736 | tf_op jit(solution)/shard_map/ppermute | solution.py:53
  141.1 55.8 %collective-permute-start.22 = (bf16[2,128,1024]{2,1,0:T(8,128)(2,1)S(1)}, bf16[2,128,1024]{2,1,0:T(8,128)(2,1)S(1)}, u32[]{:S(2)}, u32[]{:S(2)}) collective-permute-start(bf16[2,128,1024]{2,1,0:T(8,128)(2,1)S(1)} %bitcast.217), channel_id=1, source_target_pairs={{0,16},{8,56},{1,17},{9,57},{2,18},{10,58},{3,19},{11,59},{64,80},... | collective-permute-start | bytes 1572872 | tf_op jit(solution)/shard_map/ppermute | solution.py:53
  145.1 16.2 %collective-permute-start.28 = (bf16[2,256,1024]{2,1,0:T(8,128)(2,1)}, bf16[2,256,1024]{2,1,0:T(8,128)(2,1)S(1)}, u32[]{:S(2)}, u32[]{:S(2)}) collective-permute-start(bf16[2,256,1024]{2,1,0:T(8,128)(2,1)} %collective-permute-done.27), channel_id=1, source_target_pairs={{0,1},{8,11},{1,2},{9,8},{2,3},{10,9},{3,0},{11,10},{64,65},{72,75... | collective-permute-start | bytes 3145736 | tf_op jit(solution)/shard_map/ppermute | solution.py:53
  194.4 58.1 %collective-permute-start.36 = (f32[8,128,1024]{2,1,0:T(8,128)S(1)}, f32[8,128,1024]{2,1,0:T(8,128)}, u32[]{:S(2)}, u32[]{:S(2)}) collective-permute-start(f32[8,128,1024]{2,1,0:T(8,128)S(1)} %get-tuple-element.45), channel_id=1, source_target_pairs={{0,8},{8,0},{1,9},{9,1},{2,10},{10,2},{3,11},{11,3},{64,72},{72,64... | collective-permute-start | bytes 12582920 | tf_op jit(solution)/shard_map/ppermute | solution.py:53
  194.6 10.5 %collective-permute-start.8 = (bf16[2,128,1024]{2,1,0:T(8,128)(2,1)S(1)}, bf16[2,128,1024]{2,1,0:T(8,128)(2,1)S(1)}, u32[]{:S(2)}, u32[]{:S(2)}) collective-permute-start(bf16[2,128,1024]{2,1,0:T(8,128)(2,1)S(1)} %bitcast.218), channel_id=1, source_target_pairs={{0,16},{8,56},{1,17},{9,57},{2,18},{10,58},{3,19},{11,59},{64,80},... | collective-permute-start | bytes 1572872 | tf_op jit(solution)/shard_map/ppermute | solution.py:53
  197.2 13.5 %collective-permute-start.23 = (bf16[2,128,1024]{2,1,0:T(8,128)(2,1)S(1)}, bf16[2,128,1024]{2,1,0:T(8,128)(2,1)S(1)}, u32[]{:S(2)}, u32[]{:S(2)}) collective-permute-start(bf16[2,128,1024]{2,1,0:T(8,128)(2,1)S(1)} %fusion.3), channel_id=1, source_target_pairs={{0,16},{8,56},{1,17},{9,57},{2,18},{10,58},{3,19},{11,59},{64,80},... | collective-permute-start | bytes 1572872 | tf_op jit(solution)/shard_map/ppermute | solution.py:53
  205.3 11.0 %collective-permute-start.9 = (bf16[2,128,1024]{2,1,0:T(8,128)(2,1)S(1)}, bf16[2,128,1024]{2,1,0:T(8,128)(2,1)S(1)}, u32[]{:S(2)}, u32[]{:S(2)}) collective-permute-start(bf16[2,128,1024]{2,1,0:T(8,128)(2,1)S(1)} %fusion.5), channel_id=1, source_target_pairs={{0,16},{8,56},{1,17},{9,57},{2,18},{10,58},{3,19},{11,59},{64,80},... | collective-permute-start | bytes 1572872 | tf_op jit(solution)/shard_map/ppermute | solution.py:53
  210.9 11.0 %collective-permute-start.24 = (bf16[2,128,1024]{2,1,0:T(8,128)(2,1)S(1)}, bf16[2,128,1024]{2,1,0:T(8,128)(2,1)S(1)}, u32[]{:S(2)}, u32[]{:S(2)}) collective-permute-start(bf16[2,128,1024]{2,1,0:T(8,128)(2,1)S(1)} %fusion.2), channel_id=1, source_target_pairs={{0,16},{8,56},{1,17},{9,57},{2,18},{10,58},{3,19},{11,59},{64,80},... | collective-permute-start | bytes 1572872 | tf_op jit(solution)/shard_map/ppermute | solution.py:53
  216.5 18.3 %collective-permute-start.10 = (bf16[2,128,1024]{2,1,0:T(8,128)(2,1)S(1)}, bf16[2,128,1024]{2,1,0:T(8,128)(2,1)S(1)}, u32[]{:S(2)}, u32[]{:S(2)}) collective-permute-start(bf16[2,128,1024]{2,1,0:T(8,128)(2,1)S(1)} %fusion.4), channel_id=1, source_target_pairs={{0,16},{8,56},{1,17},{9,57},{2,18},{10,58},{3,19},{11,59},{64,80},... | collective-permute-start | bytes 1572872 | tf_op jit(solution)/shard_map/ppermute | solution.py:53
  217.7 12.7 %collective-permute-start.29 = (bf16[128,1024]{1,0:T(8,128)(2,1)S(1)}, bf16[128,1024]{1,0:T(8,128)(2,1)S(1)}, u32[]{:S(2)}, u32[]{:S(2)}) collective-permute-start(bf16[128,1024]{1,0:T(8,128)(2,1)S(1)} %get-tuple-element.64), channel_id=1, source_target_pairs={{0,16},{8,56},{1,17},{9,57},{2,18},{10,58},{3,19},{11,59},{64,80},... | collective-permute-start | bytes 786440 | tf_op jit(solution)/shard_map/ppermute | solution.py:53
  218.0 15.2 %collective-permute-start.33 = (bf16[128,1024]{1,0:T(8,128)(2,1)S(1)}, bf16[128,1024]{1,0:T(8,128)(2,1)S(1)}, u32[]{:S(2)}, u32[]{:S(2)}) collective-permute-start(bf16[128,1024]{1,0:T(8,128)(2,1)S(1)} %fusion.12), channel_id=1, source_target_pairs={{0,16},{8,56},{1,17},{9,57},{2,18},{10,58},{3,19},{11,59},{64,80},... | collective-permute-start | bytes 786440 | tf_op jit(solution)/shard_map/ppermute | solution.py:53
  222.2 22.6 %collective-permute-start.25 = (bf16[128,1024]{1,0:T(8,128)(2,1)S(1)}, bf16[128,1024]{1,0:T(8,128)(2,1)S(1)}, u32[]{:S(2)}, u32[]{:S(2)}) collective-permute-start(bf16[128,1024]{1,0:T(8,128)(2,1)S(1)} %fusion.18), channel_id=1, source_target_pairs={{0,64},{8,72},{1,65},{9,73},{2,66},{10,74},{3,67},{11,75},{64,0},{... | collective-permute-start | bytes 786440 | tf_op jit(solution)/shard_map/ppermute | solution.py:53
  263.0 10.8 %all-to-all-start.1 = ((f32[8,1,128]{2,1,0:T(1,128)}), f32[8,1,128]{2,1,0:T(1,128)S(1)}, u32[]{:S(2)}, u32[]{:S(2)}) async-start(f32[8,1,128]{2,1,0:T(1,128)} %get-tuple-element.39), calls=%async_computation.1 | async-start | bytes 8192 | tf_op jit(solution)/shard_map/all_to_all | solution.py:299
  (23 other events, 176.0 us)
